TPU v7x, 1024 devices: a whole 4x8x16 slice. The times are simulated.
1024 devices in a mesh: section: 32 (over y, z_hi, core), dp: 32 (over z_lo, x).
Axes of the slice: x: 4, y: 8, z: 16 (z_hi: 2, z_lo: 8; z = z_hi * 8 + z_lo), core: 2. Of those that a mesh axis runs over, the one named last changes fastest.
Arguments:
- latents: bfloat16 [6, 704, 1536], P(None, 'dp'), may hold values from -6 to 6
- control_hint: bfloat16 [6, 704, 1536], P(None, 'dp'), may hold values from -6 to 6
- upstream: bfloat16 [6, 704, 1536], P(None, 'dp'), may hold values from -6 to 6
- batch_order: int32 [6], replicated, may hold values from 0 to 5, each once
- section_weight: bfloat16 [32, 1536, 1536], P('section'), may hold values from -0.078125 to 0.078125
- zero_weight: bfloat16 [32, 768, 1536], P('section'), may hold values from -0.0390625 to 0.0390625
Outputs:
- zero_grad: float32 [32, 768, 1536], P('section', 'dp')
Inputs may be any that keep to these rules, and one draw needn't show every extreme that they name: batch_order names each of the 6 micro-batches exactly once.
All inputs are finite; a program needn't handle non-finite values.
Results may differ from a plain program's by a relative error of at most 0.03.
Values may be sent and summed in bfloat16 or wider, within the bound.
No kernel may reach another device: no remote copies, remote signals or barrier semaphores. Data moves between devices by JAX's collectives and lax.ppermute only.
A program may use at most 32 MiB of HBM per device.

v0:
```python
import math

import jax
import jax.numpy as jnp
from jax import lax
from jax.sharding import PartitionSpec as P

tanh_coef = 0.7978845608028654
cube_coef = 0.044715


def shifted(value, axis, steps):
    count = lax.axis_size(axis)
    initial, last = (max(0, -steps), min(count, count - steps))
    return lax.ppermute(value, axis, [(source, source + steps) for source in range(initial, last)])


def gelu_value(values):
    inner = tanh_coef * (values + cube_coef * values * values * values)
    return 0.5 * values * (1.0 + jnp.tanh(inner))


def gelu_slope(values):
    inner = tanh_coef * (values + cube_coef * values * values * values)
    tangent = jnp.tanh(inner)
    return 0.5 * (1.0 + tangent) + 0.5 * values * (1.0 - tangent * tangent) * tanh_coef * (
        1.0 + 3.0 * cube_coef * values * values
    )


def keep_row(stored, incoming, active, slot_index):
    previous = lax.dynamic_index_in_dim(stored, slot_index, 0, keepdims=False)
    return lax.dynamic_update_index_in_dim(
        stored, jnp.where(active, incoming, previous), slot_index, 0
    )


def send_down(message):
    return shifted(message, "section", -1)


def body(latents, control_hint, upstream, batch_order, section_weight, zero_weight):
    section_count = lax.axis_size("section")
    block_count = section_count // 2
    section_place = lax.axis_index("section")
    section_depth = section_place // 2
    is_base = section_place % 2 == 0
    weight = section_weight[0]
    zero_rows = zero_weight[0]
    model_width = weight.shape[0]
    half_width = zero_rows.shape[0]
    micro_count = latents.shape[0]
    row_count = latents.shape[1]
    ordered = jnp.take(latents, batch_order, axis=0)
    hinted = jnp.take(control_hint, batch_order, axis=0)
    started = (ordered.astype(jnp.float32) + hinted.astype(jnp.float32)).astype(jnp.bfloat16)
    first_input = jnp.where(is_base, ordered, started)

    def control_work(inputs_now):
        product = jnp.dot(inputs_now, weight, preferred_element_type=jnp.float32)
        control_state = (inputs_now.astype(jnp.float32) + gelu_value(product)).astype(jnp.bfloat16)
        partial_residual = jnp.dot(
            control_state[:, half_width:], zero_rows, preferred_element_type=jnp.float32
        ).astype(jnp.bfloat16)
        message = jnp.concatenate([control_state[:, :half_width], partial_residual], axis=1)
        return (control_state, message, control_state[:, half_width:])

    def control_spare(inputs_now):
        return (
            jnp.zeros_like(inputs_now),
            jnp.zeros((row_count, half_width + model_width), jnp.bfloat16),
            jnp.zeros((row_count, half_width), jnp.bfloat16),
        )

    def base_work(inputs_now, message):
        product = jnp.dot(inputs_now, weight, preferred_element_type=jnp.float32)
        residual_add = jnp.dot(
            message[:, :half_width], zero_rows, preferred_element_type=jnp.float32
        ) + message[:, half_width:].astype(jnp.float32)
        stream_next = (inputs_now.astype(jnp.float32) + gelu_value(product) + residual_add).astype(
            jnp.bfloat16
        )
        return (stream_next, gelu_slope(product), message[:, :half_width])

    def base_spare(inputs_now, message):
        return (
            jnp.zeros_like(inputs_now),
            jnp.zeros((row_count, model_width), jnp.float32),
            jnp.zeros((row_count, half_width), jnp.bfloat16),
        )

    def forward_step(step_index, loop_state):
        chain_in, slopes, side_rows = loop_state
        own_slot = step_index - section_depth
        active = (own_slot >= 0) & (own_slot < micro_count)
        slot_index = jnp.clip(own_slot, 0, micro_count - 1)
        inputs_now = jnp.where(
            section_depth == 0,
            lax.dynamic_index_in_dim(first_input, slot_index, 0, keepdims=False),
            chain_in,
        )
        control_out, message, control_side = lax.cond(
            active & jnp.logical_not(is_base), control_work, control_spare, inputs_now
        )
        received = send_down(message)
        base_out, slope_rows, base_side = lax.cond(
            active & is_base, base_work, base_spare, inputs_now, received
        )
        outgoing = jnp.where(is_base, base_out, control_out)
        slopes = keep_row(slopes, slope_rows, active & is_base, slot_index)
        side_rows = keep_row(
            side_rows, jnp.where(is_base, base_side, control_side), active, slot_index
        )
        chain_in = shifted(outgoing, "section", 2)
        return (chain_in, slopes, side_rows)

    forward_start = (
        jnp.zeros((row_count, model_width), jnp.bfloat16),
        jnp.zeros((micro_count, row_count, model_width), jnp.float32),
        jnp.zeros((micro_count, row_count, half_width), jnp.bfloat16),
    )
    chain_end, slopes, side_rows = lax.fori_loop(
        0, block_count + micro_count - 1, forward_step, forward_start
    )

    def pass_back(grad_in, slope_rows):
        scaled = (grad_in.astype(jnp.float32) * slope_rows).astype(jnp.bfloat16)
        back_term = jnp.dot(scaled, weight.T, preferred_element_type=jnp.float32)
        return (grad_in.astype(jnp.float32) + back_term).astype(jnp.bfloat16)

    def pass_spare(grad_in, slope_rows):
        return jnp.zeros_like(grad_in)

    back_offset = section_count - 1 - section_place

    def backward_step(step_index, loop_state):
        chain_in, grad_rows = loop_state
        own_slot = step_index - back_offset
        active = (own_slot >= 0) & (own_slot < micro_count)
        slot_index = jnp.clip(own_slot, 0, micro_count - 1)
        grad_in = jnp.where(
            section_place == section_count - 1,
            lax.dynamic_index_in_dim(upstream, slot_index, 0, keepdims=False),
            chain_in,
        )
        slope_rows = lax.dynamic_index_in_dim(slopes, slot_index, 0, keepdims=False)
        passed = lax.cond(
            active & is_base & (section_depth > 0), pass_back, pass_spare, grad_in, slope_rows
        )
        outgoing = jnp.where(is_base, passed, grad_in)
        grad_rows = keep_row(grad_rows, grad_in, active, slot_index)
        chain_in = send_down(outgoing)
        return (chain_in, grad_rows)

    backward_start = (
        jnp.zeros((row_count, model_width), jnp.bfloat16),
        jnp.zeros((micro_count, row_count, model_width), jnp.bfloat16),
    )
    back_end, grad_rows = lax.fori_loop(
        0, section_count + micro_count - 1, backward_step, backward_start
    )
    side_flat = side_rows.reshape(-1, half_width)
    grad_flat = grad_rows.reshape(-1, model_width)
    partial_value = jnp.einsum(
        "rs,rd->sd", side_flat, grad_flat, preferred_element_type=jnp.float32
    )
    summed = lax.psum_scatter(
        partial_value[None].astype(jnp.bfloat16), "dp", scatter_dimension=1, tiled=True
    ).astype(jnp.float32)
    grad_scale = 1.0 / math.sqrt(micro_count * row_count * lax.axis_size("dp"))
    return summed * grad_scale


def solution(mesh):
    placed = (
        P(None, "dp", None),
        P(None, "dp", None),
        P(None, "dp", None),
        P(),
        P("section", None, None),
        P("section", None, None),
    )
    return jax.shard_map(
        body, mesh=mesh, in_specs=placed, out_specs=P("section", "dp", None), check_vma=False
    )
```

profile of v0, /device:TPU:1, one launch (start us, length us, event | category | flops | bytes accessed | tf_op | source)
XLA Modules:
  0.0 1662.3 jit_solution(17330801279617002084)
XLA Ops:
  10.5 735.8 %while.35 = (s32[]{:T(128)}, bf16[22,1536]{1,0:T(8,128)(2,1)S(1)}, f32[6,22,1536]{2,1,0:T(8,128)S(1)}, bf16[6,22,768]{2,1,0:T(8,128)(2,1)S(1)}, pred[]{:T(512)},...) while((s32[]{:T(128)}, bf16[22,1536]{1,0:T(8,128)(2,1)S(1)}, ...), condition=%wide.region_5.7_spmd, body=%wide.region_0.6_spmd.sunk | while | flops 313218048 | bytes 36385240 | solution.py:122
  73.6 14.7 collective-permute-start.1
  112.5 13.4 collective-permute-start.1
  257.8 18.5 %collective-permute-start.1 = (bf16[22,1536]{1,0:T(8,128)(2,1)S(1)}, bf16[22,1536]{1,0:T(8,128)(2,1)S(1)}, u32[]{:S(2)}, u32[]{:S(2)}) collective-permute-start(bf16[22,1536]{1,0:T(8,128)(2,1)S(1)} %broadcast_select_fusion.4), channel_id=1, source_target_pairs={{0,64},{32,96},{64,128},{96,160},{128,192},{160,224},{192,256},{22... | collective-permute-start | bytes 202760 | tf_op jit(solution)/shard_map/while/body/eval_jaxpr/ppermute | solution.py:15
  345.6 13.4 collective-permute-done
  378.2 13.6 collective-permute-done
  393.3 13.7 collective-permute-start.1
  426.0 13.7 collective-permute-start.1
  458.7 14.1 collective-permute-start.1
  491.8 13.9 collective-permute-start.1
  524.8 13.7 collective-permute-start.1
  557.7 14.2 collective-permute-start.1
  577.1 13.8 collective-permute-done
  592.5 13.6 collective-permute-start.1
  611.4 13.7 collective-permute-done
  626.7 15.5 collective-permute-start.1
  661.7 14.5 collective-permute-start.1
  695.4 14.3 collective-permute-start.1
  729.7 15.2 collective-permute-start.1
  746.3 595.7 %while.36 = (s32[]{:T(128)}, bf16[22,1536]{1,0:T(8,128)(2,1)S(1)}, bf16[6,22,1536]{2,1,0:T(8,128)(2,1)S(1)}, pred[]{:T(512)}, s32[]{:T(128)}, /*index=5*/pred[]{...) while((s32[]{:T(128)}, bf16[22,1536]{1,0:T(8,128)(2,1)S(1)}, ...), condition=%wide.region_9.11_spmd, body=%wide.region_6.10_spmd.sunk | while | flops 104113160 | bytes 6052136 | solution.py:159
  919.1 13.5 collective-permute-done.2
  935.5 13.4 collective-permute-done.2
  951.8 13.4 collective-permute-done.2
  968.0 13.4 collective-permute-done.2
  984.3 13.4 collective-permute-done.2
  1000.6 13.4 collective-permute-done.2
  1114.5 14.1 collective-permute-done.2
  1147.8 13.4 collective-permute-done.2
  1164.1 13.4 collective-permute-done.2
  1180.4 13.4 collective-permute-done.2
  1212.9 17.0 %collective-permute-done.2 = bf16[22,1536]{1,0:T(8,128)(2,1)S(1)} collective-permute-done((bf16[22,1536]{1,0:T(8,128)(2,1)S(1)}, bf16[22,1536]{1,0:T(8,128)(2,1)S(1)}, u32[]{:S(2)}, u32[]{:S(2)}) %collective-permute-start.2) | collective-permute-done | bytes 67616 | tf_op jit(solution)/shard_map/while/body/eval_jaxpr/ppermute | solution.py:15
  1344.3 309.6 %reduce-scatter.2.cloned.1.call-done = bf16[1,24,1536]{2,1,0:T(8,128)(2,1)} async-done(((bf16[1,768,1536]{2,1,0:T(8,128)(2,1)}), bf16[1,24,1536]{2,1,0:T(8,128)(2,1)}) %reduce-scatter.2.cloned.1.call-update) | async-done | bytes 73744 | tf_op jit(solution)/shard_map/reduce_scatter | solution.py:167
  (643 shorter events, 999.8 us)
Async XLA Ops:
  6.5 1647.3 %reduce-scatter.2.cloned.1.call-start = ((), (), s32[]{:S(2)}) async-start(), calls=%async_computation.1 | async-start | bytes 2433024 | tf_op jit(solution)/shard_map/reduce_scatter | solution.py:167
  17.1 17.7 %collective-permute-start = (bf16[22,2304]{1,0:T(8,128)(2,1)S(1)}, bf16[22,2304]{1,0:T(8,128)(2,1)S(1)}, u32[]{:S(2)}, u32[]{:S(2)}) collective-permute-start(bf16[22,2304]{1,0:T(8,128)(2,1)S(1)} %get-tuple-element.677), channel_id=1, source_target_pairs={{32,0},{64,32},{96,64},{128,96},{160,128},{192,160},{224,192},{256... | collective-permute-start | bytes 304136 | tf_op jit(solution)/shard_map/while/body/eval_jaxpr/ppermute | solution.py:15
  73.6 16.1 collective-permute-start.1
  257.8 19.9 %collective-permute-start.1 = (bf16[22,1536]{1,0:T(8,128)(2,1)S(1)}, bf16[22,1536]{1,0:T(8,128)(2,1)S(1)}, u32[]{:S(2)}, u32[]{:S(2)}) collective-permute-start(bf16[22,1536]{1,0:T(8,128)(2,1)S(1)} %broadcast_select_fusion.4), channel_id=1, source_target_pairs={{0,64},{32,96},{64,128},{96,160},{128,192},{160,224},{192,256},{22... | collective-permute-start | bytes 202760 | tf_op jit(solution)/shard_map/while/body/eval_jaxpr/ppermute | solution.py:15
  343.6 15.4 collective-permute-start
  376.2 15.6 collective-permute-start
  458.7 15.4 collective-permute-start.1
  491.8 15.3 collective-permute-start.1
  557.7 16.1 collective-permute-start.1
  575.2 15.8 collective-permute-start
  592.5 15.7 collective-permute-start.1
  609.4 15.7 collective-permute-start
  626.7 17.4 %collective-permute-start.1 = (bf16[22,1536]{1,0:T(8,128)(2,1)S(1)}, bf16[22,1536]{1,0:T(8,128)(2,1)S(1)}, u32[]{:S(2)}, u32[]{:S(2)}) collective-permute-start(bf16[22,1536]{1,0:T(8,128)(2,1)S(1)} %broadcast_select_fusion.4), channel_id=1, source_target_pairs={{0,64},{32,96},{64,128},{96,160},{128,192},{160,224},{192,256},{22... | collective-permute-start | bytes 202760 | tf_op jit(solution)/shard_map/while/body/eval_jaxpr/ppermute | solution.py:15
  661.7 15.9 collective-permute-start.1
  695.4 16.7 %collective-permute-start.1 = (bf16[22,1536]{1,0:T(8,128)(2,1)S(1)}, bf16[22,1536]{1,0:T(8,128)(2,1)S(1)}, u32[]{:S(2)}, u32[]{:S(2)}) collective-permute-start(bf16[22,1536]{1,0:T(8,128)(2,1)S(1)} %broadcast_select_fusion.4), channel_id=1, source_target_pairs={{0,64},{32,96},{64,128},{96,160},{128,192},{160,224},{192,256},{22... | collective-permute-start | bytes 202760 | tf_op jit(solution)/shard_map/while/body/eval_jaxpr/ppermute | solution.py:15
  729.7 16.6 collective-permute-start.1
  917.2 15.4 collective-permute-start.2
  933.6 15.3 collective-permute-start.2
  949.8 15.3 collective-permute-start.2
  966.1 15.3 collective-permute-start.2
  982.4 15.3 collective-permute-start.2
  998.7 15.3 collective-permute-start.2
  1063.7 15.3 collective-permute-start.2
  1080.0 15.3 collective-permute-start.2
  1096.3 15.3 collective-permute-start.2
  1112.6 16.1 collective-permute-start.2
  1129.6 15.3 collective-permute-start.2
  1145.9 15.3 collective-permute-start.2
  1162.2 15.3 collective-permute-start.2
  1178.4 15.3 collective-permute-start.2
  1194.7 15.3 collective-permute-start.2
  1211.0 18.9 %collective-permute-start.2 = (bf16[22,1536]{1,0:T(8,128)(2,1)S(1)}, bf16[22,1536]{1,0:T(8,128)(2,1)S(1)}, u32[]{:S(2)}, u32[]{:S(2)}) collective-permute-start(bf16[22,1536]{1,0:T(8,128)(2,1)S(1)} %broadcast_select_fusion.5), channel_id=1, source_target_pairs={{32,0},{64,32},{96,64},{128,96},{160,128},{192,160},{224,192},{256... | collective-permute-start | bytes 202760 | tf_op jit(solution)/shard_map/while/body/eval_jaxpr/ppermute | solution.py:15
  (55 other events, 742.5 us)
Sparse Core Ops, SparseCore 0:
  1344.4 309.3 reduce-scatter.1
where the time goes:
time: 1690 us; the launch traced here: 1660 us
  waiting for transfers between devices  1080 us (64%)
  starting transfers between devices  415 us (25%)
  other arithmetic  74.3 us (4%)
  local copies, waits for them, and re-layouts  44.3 us (3%)
  matrix products  32.6 us (2%)
    ppermute x79, waiting for transfers between devices, shifted(): lax.ppermute(value, axis, [(source, source + steps) for source in range(i...  769 us
    ppermute x79, starting transfers between devices, shifted(): lax.ppermute(value, axis, [(source, source + steps) for source in range(i...  415 us
    reduce_scatter x1, waiting for transfers between devices, body(): lax.psum_scatter(partial_value[None].astype(jnp.bfloat16), 'dp', scatter_...  310 us
    dynamic_update_slice x79, other arithmetic, keep_row(): lax.dynamic_update_index_in_dim(stored, jnp.where(active, incoming, previ...  51.5 us
  transfers between devices with their start and end apart: 80, of which 80 were waited for; matrix products, arithmetic and copies ran while one was open for 1% of the time, Pallas kernels for 0%

commit v1 on v0

v1 whole, which is shorter than its diff:
```python
import functools
import math

import jax
import jax.numpy as jnp
from jax import lax
from jax.experimental import pallas as pl
from jax.experimental.pallas import tpu as pltpu
from jax.sharding import PartitionSpec as P

tanh_coef = 0.7978845608028654
cube_coef = 0.044715
chunk_count = 2
x_size = 4
both_axes = ("section", "dp")


def gelu_value(values):
    inner = tanh_coef * (values + cube_coef * values * values * values)
    return 0.5 * values * (1.0 + jnp.tanh(inner))


def gelu_slope(values):
    inner = tanh_coef * (values + cube_coef * values * values * values)
    tangent = jnp.tanh(inner)
    return 0.5 * (1.0 + tangent) + 0.5 * values * (1.0 - tangent * tangent) * tanh_coef * (
        1.0 + 3.0 * cube_coef * values * values
    )


in_vmem = pl.BlockSpec(memory_space=pltpu.VMEM)
in_smem = pl.BlockSpec(memory_space=pltpu.SMEM)


def local_call(kernel, operands, results, flops, aliases, scratch=()):
    return pl.pallas_call(
        kernel,
        out_shape=results,
        in_specs=[in_smem] + [in_vmem] * (len(operands) - 1),
        out_specs=tuple([in_vmem] * len(results)),
        input_output_aliases=aliases,
        scratch_shapes=scratch,
        compiler_params=pltpu.CompilerParams(vmem_limit_bytes=4 << 20),
        cost_estimate=pl.CostEstimate(flops=flops, bytes_accessed=flops // 256, transcendentals=0),
    )(*operands)


def shape_of(value, dtype=None):
    return jax.ShapeDtypeStruct(value.shape, dtype or value.dtype)


def columns_of(index, size):
    return pl.ds(pl.multiple_of(index * size, size), size)


def in_chunks(step):
    return (step >= 0) & (step < chunk_count)


def entry_rows(depth_now, first_depth, own, arrived, chosen):
    if arrived is None:
        return own
    if own is None:
        return arrived

    @pl.when(depth_now == first_depth)
    def _():
        chosen[...] = own[...]

    @pl.when(depth_now != first_depth)
    def _():
        chosen[...] = arrived[...]

    return chosen


def layer_kernel(step, has_arrived, has_own, *refs):
    refs = list(refs)
    place = refs.pop(0)
    arrived = refs.pop(0) if has_arrived else None
    own = refs.pop(0) if has_own else None
    residual, weight, kept_in, outgoing, kept, chosen = refs
    del kept_in
    is_base, depth = place[0], place[1]
    chunk = step - 1 - depth
    inputs = entry_rows(depth, 0, own, arrived, chosen)
    width = weight.shape[1]
    size = min(256, width)

    @pl.loop(0, width // size)
    def _(index):
        part = columns_of(index, size)
        product = jnp.dot(inputs[...], weight[:, part], preferred_element_type=jnp.float32)
        added = jnp.where(is_base == 1, residual[:, part], 0.0)
        total = inputs[:, part].astype(jnp.float32) + gelu_value(product) + added
        outgoing[:, part] = total.astype(jnp.bfloat16)

        @pl.when(in_chunks(chunk))
        def _():
            kept[jnp.clip(chunk, 0, chunk_count - 1), :, part] = product


def residual_kernel(
    step, place, received, outgoing, zero_rows, second_rows, sides_in, residual, sides
):
    del sides_in
    half, width = zero_rows.shape
    size = min(256, width)
    chunk = step - place[1]
    slot = jnp.clip(chunk, 0, chunk_count - 1)

    @pl.when(place[0] == 1)
    def _():
        @pl.loop(0, width // size)
        def _(index):
            part = columns_of(index, size)
            residual[:, part] = jnp.dot(
                received[:, :half], zero_rows[:, part], preferred_element_type=jnp.float32
            ) + jnp.dot(
                received[:, half:], second_rows[:, part], preferred_element_type=jnp.float32
            )

    @pl.when((place[0] == 1) & in_chunks(chunk))
    def _():
        sides[slot] = received[:, :half]

    @pl.when((place[0] == 0) & in_chunks(chunk))
    def _():
        sides[slot] = outgoing[:, half:]


def back_kernel(step, last_depth, has_arrived, has_own, has_slopes, *refs):
    refs = list(refs)
    place = refs.pop(0)
    arrived = refs.pop(0) if has_arrived else None
    own = refs.pop(0) if has_own else None
    if has_slopes:
        slopes, weight, kept_in, outgoing, kept, chosen, scaled = refs
    else:
        kept_in, kept, chosen = refs
    del kept_in
    chunk = step - (last_depth - place[1])
    slot = jnp.clip(chunk, 0, chunk_count - 1)
    grad = entry_rows(place[1], last_depth, own, arrived, chosen)

    if has_slopes:
        width = weight.shape[1]
        size = min(256, width)
        scaled[...] = (grad[...].astype(jnp.float32) * slopes[slot]).astype(jnp.bfloat16)

        @pl.loop(0, width // size)
        def _(index):
            part = columns_of(index, size)
            back_term = lax.dot_general(
                scaled[...],
                weight[part, :],
                (((1,), (1,)), ((), ())),
                preferred_element_type=jnp.float32,
            )
            outgoing[:, part] = (grad[:, part].astype(jnp.float32) + back_term).astype(
                jnp.bfloat16
            )

    @pl.when(in_chunks(chunk))
    def _():
        kept[slot] = grad[...]


def slope_kernel(products, slopes):
    width = products.shape[-1]
    size = min(256, width)

    @pl.loop(0, width // size)
    def _(index):
        part = columns_of(index, size)
        for chunk in range(chunk_count):
            slopes[chunk, :, part] = gelu_slope(products[chunk, :, part])


def body(latents, control_hint, upstream, batch_order, section_weight, zero_weight):
    section_count = lax.axis_size("section")
    dp_count = lax.axis_size("dp")
    z_size = dp_count // x_size
    block_count = section_count // 2
    section_place = lax.axis_index("section")
    dp_place = lax.axis_index("dp")
    x_place = dp_place % x_size
    z_place = dp_place // x_size
    depth = section_place // 2
    is_base = section_place % 2 == 0
    weight = section_weight[0]
    zero_rows = zero_weight[0]
    width = weight.shape[0]
    half = zero_rows.shape[0]
    all_rows = latents.shape[0] * latents.shape[1]
    rows = all_rows // chunk_count

    def mirrored(place):
        return (z_size - 1 - place // x_size) * x_size + place % x_size

    def move(value, section_pairs, flip):
        pairs = [
            (source * dp_count + place, target * dp_count + (mirrored(place) if flip else place))
            for source, target in section_pairs
            for place in range(dp_count)
        ]
        return lax.ppermute(value, both_axes, pairs)

    def active_blocks(step):
        return [
            step - chunk for chunk in range(chunk_count) if 0 <= step - chunk < block_count
        ]

    last_base = section_count - 2
    second_rows = move(
        zero_rows, [(2 * block + 1, 2 * block) for block in range(block_count)], False
    )
    upstream_rows = move(
        upstream.reshape(all_rows, width), [(last_base, last_base)], True
    ).reshape(chunk_count, rows, width)

    ordered = jnp.take(latents, batch_order, axis=0)
    hinted = jnp.take(control_hint, batch_order, axis=0)
    started = (ordered.astype(jnp.float32) + hinted.astype(jnp.float32)).astype(jnp.bfloat16)
    first_rows = jnp.where(is_base, ordered, started).reshape(chunk_count, rows, width)

    place = jnp.stack([is_base.astype(jnp.int32), depth])
    row_buffer = pltpu.VMEM((rows, width), jnp.bfloat16)
    row_shape = jax.ShapeDtypeStruct((rows, width), jnp.bfloat16)
    arrived = None
    residual = jnp.zeros((rows, width), jnp.float32)
    products = jnp.zeros((chunk_count, rows, width), jnp.float32)
    sides = jnp.zeros((chunk_count, rows, half), jnp.bfloat16)
    for step in range(block_count + chunk_count):
        entering = ()
        if arrived is not None:
            entering += (arrived,)
        if step <= chunk_count:
            entering += (
                jnp.where(
                    is_base, first_rows[max(step - 1, 0)], first_rows[min(step, chunk_count - 1)]
                ),
            )
        outgoing, products = local_call(
            functools.partial(layer_kernel, step, arrived is not None, step <= chunk_count),
            (place,) + entering + (residual, weight, products),
            (row_shape, shape_of(products)),
            2 * rows * width * width,
            {3 + len(entering): 1},
            (row_buffer,),
        )
        hops = [
            (2 * block + 1 - lag, 2 * block + 3 - lag)
            for lag in (0, 1)
            for block in active_blocks(step - lag)
            if block + 1 < block_count
        ]
        if hops:
            arrived = move(outgoing, hops, True)
        shares = [(2 * block + 1, 2 * block) for block in active_blocks(step)]
        if shares:
            received = move(outgoing, shares, False)
            residual, sides = local_call(
                functools.partial(residual_kernel, step),
                (place, received, outgoing, zero_rows, second_rows, sides),
                (shape_of(residual), shape_of(sides)),
                256,
                {5: 1},
            )

    (slopes,) = local_call(
        lambda unused, products_in, slopes_out: slope_kernel(products_in, slopes_out),
        (place, products),
        (shape_of(products),),
        256,
        {},
    )

    def along_x(value, shift, section_pairs=None):
        sections = range(section_count) if section_pairs is None else section_pairs
        pairs = [
            (section * dp_count + z * x_size + (x + shift) % x_size, section * dp_count + z * x_size + x)
            for section in sections
            for z in range(z_size)
            for x in range(x_size)
        ]
        return lax.ppermute(value, both_axes, pairs)

    base_sections = range(0, section_count, 2)

    def spread_side(side):
        source = lax.broadcasted_iota(jnp.int32, (half, half), 0)
        target = lax.broadcasted_iota(jnp.int32, (half, half), 1)
        quarter = half // x_size
        piece = quarter // z_size
        shift = target // quarter
        within = target % quarter
        wanted = (
            (within // piece) * piece * x_size
            + ((x_place - shift) % x_size) * piece
            + within % piece
        )
        picks = (source == wanted).astype(jnp.bfloat16)
        picked = jnp.dot(side, picks, preferred_element_type=jnp.float32).astype(jnp.bfloat16)
        parts = [picked[:, shift * quarter : (shift + 1) * quarter] for shift in range(x_size)]
        return [parts[0]] + [along_x(parts[shift], shift) for shift in range(1, x_size)]

    def spread_grad(grad):
        return jnp.concatenate(
            [grad] + [along_x(grad, shift, base_sections) for shift in range(1, x_size)], axis=0
        )

    def share_grad(gathered):
        shared = move(gathered, [(2 * block, 2 * block + 1) for block in range(block_count)], False)
        return jnp.where(is_base, gathered, shared)

    grads = jnp.zeros((chunk_count, rows, width), jnp.bfloat16)
    spread_sides = None
    grad_parts = [None] * chunk_count
    for step in range(block_count + chunk_count - 1):
        if step == block_count // 2:
            sides, arrived = lax.optimization_barrier((sides, arrived))
            spread = spread_side(sides.reshape(all_rows, half))
        if step == block_count // 2 + 2:
            spread, arrived = lax.optimization_barrier((spread, arrived))
            spread_sides = [
                jnp.concatenate([part[chunk * rows : (chunk + 1) * rows] for part in spread])
                for chunk in range(chunk_count)
            ]
        entering = ()
        if step > 0:
            entering += (arrived,)
        if step < chunk_count:
            entering += (upstream_rows[step],)
        hops = [
            (2 * (block_count - 1 - back), 2 * (block_count - 2 - back))
            for back in active_blocks(step)
            if back + 1 < block_count
        ]
        done_chunk = step - (block_count - 1)
        grad_in = arrived
        if hops:
            outgoing, grads = local_call(
                functools.partial(
                    back_kernel, step, block_count - 1, step > 0, step < chunk_count, True
                ),
                (place,) + entering + (slopes, weight, grads),
                (row_shape, shape_of(grads)),
                2 * rows * width * width,
                {3 + len(entering): 1},
                (row_buffer, row_buffer),
            )
            arrived = move(outgoing, hops, True)
        if 0 <= done_chunk < chunk_count - 1:
            gathered = spread_grad(grads[done_chunk])
            gathered, arrived = lax.optimization_barrier((gathered, arrived))
        elif done_chunk >= 0:
            gathered = spread_grad(jnp.where(depth == 0, grad_in, grads[done_chunk]))
        if done_chunk >= 0:
            grad_parts[done_chunk] = lax.dot_general(
                spread_sides[done_chunk],
                share_grad(gathered),
                (((0,), (0,)), ((), ())),
                preferred_element_type=jnp.float32,
            )

    partial_value = sum(grad_parts[1:], grad_parts[0]).reshape(
        z_size, half // dp_count, width
    )
    distance = z_size // 2
    while distance:
        upper = (z_place // distance) % 2
        kept = lax.dynamic_slice_in_dim(partial_value, upper * distance, distance, 0)
        sent = lax.dynamic_slice_in_dim(partial_value, (1 - upper) * distance, distance, 0)
        pairs = [
            (place, ((place // x_size) ^ distance) * x_size + place % x_size)
            for place in range(dp_count)
        ]
        partial_value = kept + lax.ppermute(sent.astype(jnp.bfloat16), "dp", pairs).astype(
            jnp.float32
        )
        distance //= 2
    grad_scale = 1.0 / math.sqrt(all_rows * dp_count)
    return partial_value * grad_scale


def solution(mesh):
    placed = (
        P(None, "dp", None),
        P(None, "dp", None),
        P(None, "dp", None),
        P(),
        P("section", None, None),
        P("section", None, None),
    )
    return jax.shard_map(
        body, mesh=mesh, in_specs=placed, out_specs=P("section", "dp", None), check_vma=False
    )
```

time: 1690 us -> 1310 us (0.78); the launches traced: 1660 us -> 1300 us
  waiting for transfers between devices: 1080 us -> 84.1 us
  starting transfers between devices: 415 us -> 1070 us
  Pallas kernels: 0 us -> 119 us
  other arithmetic: 74.3 us -> 2.89 us
  matrix products: 32.6 us -> 2.06 us
  local copies, waits for them, and re-layouts: 44.3 us -> 23.7 us
    ppermute x79 -> x66, waiting for transfers between devices: 769 us -> 84.1 us  [the longest x3 47.6 us: body(): lax.ppermute(sent.astype(jnp.bfloat16), 'dp', pairs).astype(jnp.float32)]
    ppermute x79 -> x66, starting transfers between devices: 415 us -> 1070 us  [the longest x54 854 us: move(): return lax.ppermute(value, both_axes, pairs)]
    reduce_scatter x1 -> x0, waiting for transfers between devices: 310 us -> none  [body(): lax.psum_scatter(partial_value[None].astype(jnp.bfloat16), 'dp', scatter_...]
    pallas_call x0 -> x52, Pallas kernels: none -> 119 us  [local_call(): pl.pallas_call(kernel, out_shape=results, in_specs=[in_smem] + [in_vmem]...]
    dynamic_update_slice x79 -> x0, other arithmetic: 51.5 us -> none  [keep_row(): lax.dynamic_update_index_in_dim(stored, jnp.where(active, incoming, previ...]
    another operation x147 -> x0, local copies, waits for them, and re-layouts: 32.7 us -> none
    dot_general x13 -> x3, matrix products: 32.6 us -> 2.06 us  [the longest x2 1.1 us: body(): lax.dot_general(spread_sides[done_chunk], share_grad(gathered), (((0,), (...]
    select_n x80 -> x3, other arithmetic: 19.8 us -> 0.32 us  [the longest x1 0.26 us: body(): jnp.where(is_base, ordered, started).reshape(chunk_count, rows, width)]
  transfers between devices with their start and end apart: 80 -> 66, of which waited for: 80 -> 7; matrix products, arithmetic and copies ran while one was open for 1% -> 1% of each run, Pallas kernels for 0% -> 3%
where the time goes in v1:
time: 1310 us; the launch traced here: 1300 us
  starting transfers between devices  1070 us (82%)
  Pallas kernels  119 us (9%)
  waiting for transfers between devices  84.1 us (6%)
  local copies, waits for them, and re-layouts  23.7 us (2%)
    ppermute x54, starting transfers between devices, move(): return lax.ppermute(value, both_axes, pairs)  854 us
    ppermute x9, starting transfers between devices, along_x(): return lax.ppermute(value, both_axes, pairs)  157 us
    pallas_call x52, Pallas kernels, local_call(): pl.pallas_call(kernel, out_shape=results, in_specs=[in_smem] + [in_vmem]...  119 us
    ppermute x3, starting transfers between devices, body(): lax.ppermute(sent.astype(jnp.bfloat16), 'dp', pairs).astype(jnp.float32)  57.1 us
    ppermute x3, waiting for transfers between devices, body(): lax.ppermute(sent.astype(jnp.bfloat16), 'dp', pairs).astype(jnp.float32)  47.6 us
    ppermute x54, waiting for transfers between devices, move(): return lax.ppermute(value, both_axes, pairs)  31.7 us
  transfers between devices with their start and end apart: 66, of which 7 were waited for; matrix products, arithmetic and copies ran while one was open for 1% of the time, Pallas kernels for 3%

profile of v1, /device:TPU:1, one launch (start us, length us, event | category | flops | bytes accessed | tf_op | source)
XLA Modules:
  0.0 1300.8 jit_solution(5903103119890461619)
XLA Ops:
  0.0 29.5 %collective-permute-start.2 = (bf16[768,1536]{1,0:T(8,128)(2,1)}, bf16[768,1536]{1,0:T(8,128)(2,1)}, u32[]{:S(2)}, u32[]{:S(2)}) collective-permute-start(bf16[768,1536]{1,0:T(8,128)(2,1)} %bitcast.50), channel_id=1, source_target_pairs={{32,0},{33,1},{34,2},{35,3},{36,4},{37,5},{38,6},{39,7},{40,8},{41... | collective-permute-start | bytes 7077896 | tf_op jit(solution)/shard_map/ppermute | solution.py:207
  40.6 12.4 collective-permute-start
  69.4 10.8 collective-permute-start.3
  81.9 16.0 %collective-permute-done.3.refs_1_ = bf16[66,1536]{1,0:T(8,128)(2,1)S(1)} collective-permute-done((bf16[66,1536]{1,0:T(8,128)(2,1)S(1)}, bf16[66,1536]{1,0:T(8,128)(2,1)S(1)}, u32[]{:S(2)}, u32[]{:S(2)}) %collective-permute-start.3) | collective-permute-done | bytes 202784 | tf_op jit(solution)/shard_map/ppermute | solution.py:207
  101.0 19.9 %collective-permute-start.5 = (bf16[66,1536]{1,0:T(8,128)(2,1)S(1)}, bf16[66,1536]{1,0:T(8,128)(2,1)S(1)}, u32[]{:S(2)}, u32[]{:S(2)}) collective-permute-start(bf16[66,1536]{1,0:T(8,128)(2,1)S(1)} %get-tuple-element.123.outgoing), channel_id=1, source_target_pairs={{160,252},{161,253},{162,254},{163,255},{164,248},{165,249},{166,2... | collective-permute-start | bytes 608264 | tf_op jit(solution)/shard_map/ppermute | solution.py:207
  125.7 39.7 %collective-permute-start.7 = (bf16[66,1536]{1,0:T(8,128)(2,1)S(1)}, bf16[66,1536]{1,0:T(8,128)(2,1)S(1)}, u32[]{:S(2)}, u32[]{:S(2)}) collective-permute-start(bf16[66,1536]{1,0:T(8,128)(2,1)S(1)} %get-tuple-element.127.outgoing), channel_id=1, source_target_pairs={{224,316},{225,317},{226,318},{227,319},{228,312},{229,313},{230,3... | collective-permute-start | bytes 608264 | tf_op jit(solution)/shard_map/ppermute | solution.py:207
  170.1 37.6 %collective-permute-start.9 = (bf16[66,1536]{1,0:T(8,128)(2,1)S(1)}, bf16[66,1536]{1,0:T(8,128)(2,1)S(1)}, u32[]{:S(2)}, u32[]{:S(2)}) collective-permute-start(bf16[66,1536]{1,0:T(8,128)(2,1)S(1)} %get-tuple-element.131.outgoing), channel_id=1, source_target_pairs={{288,380},{289,381},{290,382},{291,383},{292,376},{293,377},{294,3... | collective-permute-start | bytes 608264 | tf_op jit(solution)/shard_map/ppermute | solution.py:207
  212.4 40.7 %collective-permute-start.11 = (bf16[66,1536]{1,0:T(8,128)(2,1)S(1)}, bf16[66,1536]{1,0:T(8,128)(2,1)S(1)}, u32[]{:S(2)}, u32[]{:S(2)}) collective-permute-start(bf16[66,1536]{1,0:T(8,128)(2,1)S(1)} %get-tuple-element.135.outgoing), channel_id=1, source_target_pairs={{352,444},{353,445},{354,446},{355,447},{356,440},{357,441},{358,4... | collective-permute-start | bytes 608264 | tf_op jit(solution)/shard_map/ppermute | solution.py:207
  257.8 38.6 %collective-permute-start.13 = (bf16[66,1536]{1,0:T(8,128)(2,1)S(1)}, bf16[66,1536]{1,0:T(8,128)(2,1)S(1)}, u32[]{:S(2)}, u32[]{:S(2)}) collective-permute-start(bf16[66,1536]{1,0:T(8,128)(2,1)S(1)} %get-tuple-element.139.outgoing), channel_id=1, source_target_pairs={{416,508},{417,509},{418,510},{419,511},{420,504},{421,505},{422,5... | collective-permute-start | bytes 608264 | tf_op jit(solution)/shard_map/ppermute | solution.py:207
  301.1 41.6 %collective-permute-start.15 = (bf16[66,1536]{1,0:T(8,128)(2,1)S(1)}, bf16[66,1536]{1,0:T(8,128)(2,1)S(1)}, u32[]{:S(2)}, u32[]{:S(2)}) collective-permute-start(bf16[66,1536]{1,0:T(8,128)(2,1)S(1)} %get-tuple-element.143.outgoing), channel_id=1, source_target_pairs={{480,572},{481,573},{482,574},{483,575},{484,568},{485,569},{486,5... | collective-permute-start | bytes 608264 | tf_op jit(solution)/shard_map/ppermute | solution.py:207
  347.5 39.5 %collective-permute-start.17 = (bf16[66,1536]{1,0:T(8,128)(2,1)S(1)}, bf16[66,1536]{1,0:T(8,128)(2,1)S(1)}, u32[]{:S(2)}, u32[]{:S(2)}) collective-permute-start(bf16[66,1536]{1,0:T(8,128)(2,1)S(1)} %get-tuple-element.147.outgoing), channel_id=1, source_target_pairs={{544,636},{545,637},{546,638},{547,639},{548,632},{549,633},{550,6... | collective-permute-start | bytes 608264 | tf_op jit(solution)/shard_map/ppermute | solution.py:207
  391.7 43.8 %collective-permute-start.19 = (bf16[66,1536]{1,0:T(8,128)(2,1)S(1)}, bf16[66,1536]{1,0:T(8,128)(2,1)S(1)}, u32[]{:S(2)}, u32[]{:S(2)}) collective-permute-start(bf16[66,1536]{1,0:T(8,128)(2,1)S(1)} %get-tuple-element.151.outgoing), channel_id=1, source_target_pairs={{608,700},{609,701},{610,702},{611,703},{612,696},{613,697},{614,6... | collective-permute-start | bytes 608264 | tf_op jit(solution)/shard_map/ppermute | solution.py:207
  440.3 41.7 %collective-permute-start.21 = (bf16[66,1536]{1,0:T(8,128)(2,1)S(1)}, bf16[66,1536]{1,0:T(8,128)(2,1)S(1)}, u32[]{:S(2)}, u32[]{:S(2)}) collective-permute-start(bf16[66,1536]{1,0:T(8,128)(2,1)S(1)} %get-tuple-element.155.outgoing), channel_id=1, source_target_pairs={{672,764},{673,765},{674,766},{675,767},{676,760},{677,761},{678,7... | collective-permute-start | bytes 608264 | tf_op jit(solution)/shard_map/ppermute | solution.py:207
  486.7 43.9 %collective-permute-start.23 = (bf16[66,1536]{1,0:T(8,128)(2,1)S(1)}, bf16[66,1536]{1,0:T(8,128)(2,1)S(1)}, u32[]{:S(2)}, u32[]{:S(2)}) collective-permute-start(bf16[66,1536]{1,0:T(8,128)(2,1)S(1)} %get-tuple-element.159.outgoing), channel_id=1, source_target_pairs={{736,828},{737,829},{738,830},{739,831},{740,824},{741,825},{742,8... | collective-permute-start | bytes 608264 | tf_op jit(solution)/shard_map/ppermute | solution.py:207
  535.3 40.9 %collective-permute-start.25 = (bf16[66,1536]{1,0:T(8,128)(2,1)S(1)}, bf16[66,1536]{1,0:T(8,128)(2,1)S(1)}, u32[]{:S(2)}, u32[]{:S(2)}) collective-permute-start(bf16[66,1536]{1,0:T(8,128)(2,1)S(1)} %get-tuple-element.163.outgoing), channel_id=1, source_target_pairs={{800,892},{801,893},{802,894},{803,895},{804,888},{805,889},{806,8... | collective-permute-start | bytes 608264 | tf_op jit(solution)/shard_map/ppermute | solution.py:207
  580.9 43.0 %collective-permute-start.27 = (bf16[66,1536]{1,0:T(8,128)(2,1)S(1)}, bf16[66,1536]{1,0:T(8,128)(2,1)S(1)}, u32[]{:S(2)}, u32[]{:S(2)}) collective-permute-start(bf16[66,1536]{1,0:T(8,128)(2,1)S(1)} %get-tuple-element.167.outgoing), channel_id=1, source_target_pairs={{864,956},{865,957},{866,958},{867,959},{868,952},{869,953},{870,9... | collective-permute-start | bytes 608264 | tf_op jit(solution)/shard_map/ppermute | solution.py:207
  629.0 39.4 %collective-permute-start.30 = (bf16[66,1536]{1,0:T(8,128)(2,1)S(1)}, bf16[66,1536]{1,0:T(8,128)(2,1)}, u32[]{:S(2)}, u32[]{:S(2)}) collective-permute-start(bf16[66,1536]{1,0:T(8,128)(2,1)S(1)} %get-tuple-element.171.outgoing), channel_id=1, source_target_pairs={{928,896},{929,897},{930,898},{931,899},{932,900},{933,901},{934,9... | collective-permute-start | bytes 608264 | tf_op jit(solution)/shard_map/ppermute | solution.py:207
  668.4 23.1 %collective-permute-start.29 = (bf16[66,1536]{1,0:T(8,128)(2,1)S(1)}, bf16[66,1536]{1,0:T(8,128)(2,1)S(1)}, u32[]{:S(2)}, u32[]{:S(2)}) collective-permute-start(bf16[66,1536]{1,0:T(8,128)(2,1)S(1)} %get-tuple-element.171.outgoing), channel_id=1, source_target_pairs={{928,1020},{929,1021},{930,1022},{931,1023},{932,1016},{933,1017},... | collective-permute-start | bytes 608264 | tf_op jit(solution)/shard_map/ppermute | solution.py:207
  700.6 38.0 %collective-permute-start.32 = (bf16[66,1536]{1,0:T(8,128)(2,1)S(1)}, bf16[66,1536]{1,0:T(8,128)(2,1)S(1)}, u32[]{:S(2)}, u32[]{:S(2)}) collective-permute-start(bf16[66,1536]{1,0:T(8,128)(2,1)S(1)} %get-tuple-element.175.outgoing), channel_id=1, source_target_pairs={{992,960},{993,961},{994,962},{995,963},{996,964},{997,965},{998,9... | collective-permute-start | bytes 608264 | tf_op jit(solution)/shard_map/ppermute | solution.py:207
  738.7 23.1 %collective-permute-start.31 = (bf16[66,1536]{1,0:T(8,128)(2,1)S(1)}, bf16[66,1536]{1,0:T(8,128)(2,1)S(1)}, u32[]{:S(2)}, u32[]{:S(2)}) collective-permute-start(bf16[66,1536]{1,0:T(8,128)(2,1)S(1)} %get-tuple-element.175.outgoing), channel_id=1, source_target_pairs={{928,1020},{929,1021},{930,1022},{931,1023},{932,1016},{933,1017},... | collective-permute-start | bytes 608264 | tf_op jit(solution)/shard_map/ppermute | solution.py:207
  781.8 51.5 %collective-permute-start.37 = (bf16[66,1536]{1,0:T(8,128)(2,1)S(1)}, bf16[66,1536]{1,0:T(8,128)(2,1)S(1)}, u32[]{:S(2)}, u32[]{:S(2)}) collective-permute-start(bf16[66,1536]{1,0:T(8,128)(2,1)S(1)} %get-tuple-element.187), channel_id=1, source_target_pairs={{896,860},{897,861},{898,862},{899,863},{900,856},{901,857},{902,8... | collective-permute-start | bytes 608264 | tf_op jit(solution)/shard_map/ppermute | solution.py:207
  868.9 105.4 %collective-permute-start.44 = (bf16[132,192]{1,0:T(8,128)(2,1)S(1)}, bf16[132,192]{1,0:T(8,128)(2,1)S(1)}, u32[]{:S(2)}, u32[]{:S(2)}) collective-permute-start(bf16[132,192]{1,0:T(8,128)(2,1)S(1)} %get-tuple-element.232), channel_id=1, source_target_pairs={{1,0},{2,1},{3,2},{0,3},{5,4},{6,5},{7,6},{4,7},{9,8},{10,9},{11,1... | collective-permute-start | bytes 152072 | tf_op jit(solution)/shard_map/ppermute | solution.py:287
  974.4 23.7 %collective-permute-start.45 = (bf16[132,192]{1,0:T(8,128)(2,1)S(1)}, bf16[132,192]{1,0:T(8,128)(2,1)S(1)}, u32[]{:S(2)}, u32[]{:S(2)}) collective-permute-start(bf16[132,192]{1,0:T(8,128)(2,1)S(1)} %get-tuple-element.231), channel_id=1, source_target_pairs={{2,0},{3,1},{0,2},{1,3},{6,4},{7,5},{4,6},{5,7},{10,8},{11,9},{8,1... | collective-permute-start | bytes 152072 | tf_op jit(solution)/shard_map/ppermute | solution.py:287
  998.1 23.7 %collective-permute-start.46 = (bf16[132,192]{1,0:T(8,128)(2,1)S(1)}, bf16[132,192]{1,0:T(8,128)(2,1)S(1)}, u32[]{:S(2)}, u32[]{:S(2)}) collective-permute-start(bf16[132,192]{1,0:T(8,128)(2,1)S(1)} %get-tuple-element.230), channel_id=1, source_target_pairs={{3,0},{0,1},{1,2},{2,3},{7,4},{4,5},{5,6},{6,7},{11,8},{8,9},{9,10... | collective-permute-start | bytes 152072 | tf_op jit(solution)/shard_map/ppermute | solution.py:287
  1052.4 107.5 %collective-permute-start.62 = (bf16[264,1536]{1,0:T(8,128)(2,1)S(1)}, bf16[264,1536]{1,0:T(8,128)(2,1)S(1)}, u32[]{:S(2)}, u32[]{:S(2)}) collective-permute-start(bf16[264,1536]{1,0:T(8,128)(2,1)S(1)} %pad_maximum_fusion.1), channel_id=1, source_target_pairs={{0,32},{1,33},{2,34},{3,35},{4,36},{5,37},{6,38},{7,39},{8,40},{9,... | collective-permute-start | bytes 2433032 | tf_op jit(solution)/shard_map/ppermute | solution.py:207
  1159.9 23.8 %collective-permute-start.58 = (bf16[264,1536]{1,0:T(8,128)(2,1)S(1)}, bf16[264,1536]{1,0:T(8,128)(2,1)S(1)}, u32[]{:S(2)}, u32[]{:S(2)}) collective-permute-start(bf16[264,1536]{1,0:T(8,128)(2,1)S(1)} %pad_maximum_fusion), channel_id=1, source_target_pairs={{0,32},{1,33},{2,34},{3,35},{4,36},{5,37},{6,38},{7,39},{8,40},{9,... | collective-permute-start | bytes 2433032 | tf_op jit(solution)/shard_map/ppermute | solution.py:207
  1184.3 10.3 collective-permute-done.58
  1195.2 15.4 %collective-permute-start.63 = (bf16[4,24,1536]{2,1,0:T(8,128)(2,1)S(1)}, bf16[4,24,1536]{2,1,0:T(8,128)(2,1)S(1)}, u32[]{:S(2)}, u32[]{:S(2)}) collective-permute-start(bf16[4,24,1536]{2,1,0:T(8,128)(2,1)S(1)} %dynamic-slice_convert_fusion), channel_id=1, source_target_pairs={{0,16},{1,17},{2,18},{3,19},{4,20},{5,21},{6,22},{7,23},{8,24},{9,... | collective-permute-start | bytes 884744 | tf_op jit(solution)/shard_map/ppermute | solution.py:379
  1210.6 33.3 %collective-permute-done.63 = bf16[4,24,1536]{2,1,0:T(8,128)(2,1)S(1)} collective-permute-done((bf16[4,24,1536]{2,1,0:T(8,128)(2,1)S(1)}, bf16[4,24,1536]{2,1,0:T(8,128)(2,1)S(1)}, u32[]{:S(2)}, u32[]{:S(2)}) %collective-permute-start.63) | collective-permute-done | bytes 294944 | tf_op jit(solution)/shard_map/ppermute | solution.py:379
  1244.0 19.3 %collective-permute-start.64 = (bf16[2,24,1536]{2,1,0:T(8,128)(2,1)S(1)}, bf16[2,24,1536]{2,1,0:T(8,128)(2,1)S(1)}, u32[]{:S(2)}, u32[]{:S(2)}) collective-permute-start(bf16[2,24,1536]{2,1,0:T(8,128)(2,1)S(1)} %dynamic-slice_convert_fusion.1), channel_id=1, source_target_pairs={{0,8},{1,9},{2,10},{3,11},{4,12},{5,13},{6,14},{7,15},{8,0},{9,1},... | collective-permute-start | bytes 442376 | tf_op jit(solution)/shard_map/ppermute | solution.py:379
  1263.4 10.2 collective-permute-done.64
  1273.7 22.4 %collective-permute-start.65 = (bf16[1,24,1536]{2,1,0:T(8,128)(2,1)S(1)}, bf16[1,24,1536]{2,1,0:T(8,128)(2,1)S(1)}, u32[]{:S(2)}, u32[]{:S(2)}) collective-permute-start(bf16[1,24,1536]{2,1,0:T(8,128)(2,1)S(1)} %dynamic-slice_convert_fusion.2), channel_id=1, source_target_pairs={{0,4},{1,5},{2,6},{3,7},{4,0},{5,1},{6,2},{7,3},{8,12},{9,13},{10,... | collective-permute-start | bytes 221192 | tf_op jit(solution)/shard_map/ppermute | solution.py:379
  (230 shorter events, 189.3 us)
Async XLA Ops:
  0.0 56.1 %collective-permute-start.2 = (bf16[768,1536]{1,0:T(8,128)(2,1)}, bf16[768,1536]{1,0:T(8,128)(2,1)}, u32[]{:S(2)}, u32[]{:S(2)}) collective-permute-start(bf16[768,1536]{1,0:T(8,128)(2,1)} %bitcast.50), channel_id=1, source_target_pairs={{32,0},{33,1},{34,2},{35,3},{36,4},{37,5},{38,6},{39,7},{40,8},{41... | collective-permute-start | bytes 7077896 | tf_op jit(solution)/shard_map/ppermute | solution.py:207
  125.0 40.4 %collective-permute-start.8 = (bf16[66,1536]{1,0:T(8,128)(2,1)S(1)}, bf16[66,1536]{1,0:T(8,128)(2,1)S(1)}, u32[]{:S(2)}, u32[]{:S(2)}) collective-permute-start(bf16[66,1536]{1,0:T(8,128)(2,1)S(1)} %get-tuple-element.127.outgoing), channel_id=1, source_target_pairs={{224,192},{225,193},{226,194},{227,195},{228,196},{229,197},{230,1... | collective-permute-start | bytes 608264 | tf_op jit(solution)/shard_map/ppermute | solution.py:207
  125.7 41.4 %collective-permute-start.7 = (bf16[66,1536]{1,0:T(8,128)(2,1)S(1)}, bf16[66,1536]{1,0:T(8,128)(2,1)S(1)}, u32[]{:S(2)}, u32[]{:S(2)}) collective-permute-start(bf16[66,1536]{1,0:T(8,128)(2,1)S(1)} %get-tuple-element.127.outgoing), channel_id=1, source_target_pairs={{224,316},{225,317},{226,318},{227,319},{228,312},{229,313},{230,3... | collective-permute-start | bytes 608264 | tf_op jit(solution)/shard_map/ppermute | solution.py:207
  169.4 38.3 %collective-permute-start.10 = (bf16[66,1536]{1,0:T(8,128)(2,1)S(1)}, bf16[66,1536]{1,0:T(8,128)(2,1)S(1)}, u32[]{:S(2)}, u32[]{:S(2)}) collective-permute-start(bf16[66,1536]{1,0:T(8,128)(2,1)S(1)} %get-tuple-element.131.outgoing), channel_id=1, source_target_pairs={{288,256},{289,257},{290,258},{291,259},{292,260},{293,261},{294,2... | collective-permute-start | bytes 608264 | tf_op jit(solution)/shard_map/ppermute | solution.py:207
  170.1 39.3 %collective-permute-start.9 = (bf16[66,1536]{1,0:T(8,128)(2,1)S(1)}, bf16[66,1536]{1,0:T(8,128)(2,1)S(1)}, u32[]{:S(2)}, u32[]{:S(2)}) collective-permute-start(bf16[66,1536]{1,0:T(8,128)(2,1)S(1)} %get-tuple-element.131.outgoing), channel_id=1, source_target_pairs={{288,380},{289,381},{290,382},{291,383},{292,376},{293,377},{294,3... | collective-permute-start | bytes 608264 | tf_op jit(solution)/shard_map/ppermute | solution.py:207
  211.7 41.4 %collective-permute-start.12 = (bf16[66,1536]{1,0:T(8,128)(2,1)S(1)}, bf16[66,1536]{1,0:T(8,128)(2,1)S(1)}, u32[]{:S(2)}, u32[]{:S(2)}) collective-permute-start(bf16[66,1536]{1,0:T(8,128)(2,1)S(1)} %get-tuple-element.135.outgoing), channel_id=1, source_target_pairs={{352,320},{353,321},{354,322},{355,323},{356,324},{357,325},{358,3... | collective-permute-start | bytes 608264 | tf_op jit(solution)/shard_map/ppermute | solution.py:207
  212.4 42.4 %collective-permute-start.11 = (bf16[66,1536]{1,0:T(8,128)(2,1)S(1)}, bf16[66,1536]{1,0:T(8,128)(2,1)S(1)}, u32[]{:S(2)}, u32[]{:S(2)}) collective-permute-start(bf16[66,1536]{1,0:T(8,128)(2,1)S(1)} %get-tuple-element.135.outgoing), channel_id=1, source_target_pairs={{352,444},{353,445},{354,446},{355,447},{356,440},{357,441},{358,4... | collective-permute-start | bytes 608264 | tf_op jit(solution)/shard_map/ppermute | solution.py:207
  257.1 39.3 %collective-permute-start.14 = (bf16[66,1536]{1,0:T(8,128)(2,1)S(1)}, bf16[66,1536]{1,0:T(8,128)(2,1)S(1)}, u32[]{:S(2)}, u32[]{:S(2)}) collective-permute-start(bf16[66,1536]{1,0:T(8,128)(2,1)S(1)} %get-tuple-element.139.outgoing), channel_id=1, source_target_pairs={{416,384},{417,385},{418,386},{419,387},{420,388},{421,389},{422,3... | collective-permute-start | bytes 608264 | tf_op jit(solution)/shard_map/ppermute | solution.py:207
  257.8 40.3 %collective-permute-start.13 = (bf16[66,1536]{1,0:T(8,128)(2,1)S(1)}, bf16[66,1536]{1,0:T(8,128)(2,1)S(1)}, u32[]{:S(2)}, u32[]{:S(2)}) collective-permute-start(bf16[66,1536]{1,0:T(8,128)(2,1)S(1)} %get-tuple-element.139.outgoing), channel_id=1, source_target_pairs={{416,508},{417,509},{418,510},{419,511},{420,504},{421,505},{422,5... | collective-permute-start | bytes 608264 | tf_op jit(solution)/shard_map/ppermute | solution.py:207
  300.4 42.3 %collective-permute-start.16 = (bf16[66,1536]{1,0:T(8,128)(2,1)S(1)}, bf16[66,1536]{1,0:T(8,128)(2,1)S(1)}, u32[]{:S(2)}, u32[]{:S(2)}) collective-permute-start(bf16[66,1536]{1,0:T(8,128)(2,1)S(1)} %get-tuple-element.143.outgoing), channel_id=1, source_target_pairs={{480,448},{481,449},{482,450},{483,451},{484,452},{485,453},{486,4... | collective-permute-start | bytes 608264 | tf_op jit(solution)/shard_map/ppermute | solution.py:207
  301.1 43.4 %collective-permute-start.15 = (bf16[66,1536]{1,0:T(8,128)(2,1)S(1)}, bf16[66,1536]{1,0:T(8,128)(2,1)S(1)}, u32[]{:S(2)}, u32[]{:S(2)}) collective-permute-start(bf16[66,1536]{1,0:T(8,128)(2,1)S(1)} %get-tuple-element.143.outgoing), channel_id=1, source_target_pairs={{480,572},{481,573},{482,574},{483,575},{484,568},{485,569},{486,5... | collective-permute-start | bytes 608264 | tf_op jit(solution)/shard_map/ppermute | solution.py:207
  346.8 40.2 %collective-permute-start.18 = (bf16[66,1536]{1,0:T(8,128)(2,1)S(1)}, bf16[66,1536]{1,0:T(8,128)(2,1)S(1)}, u32[]{:S(2)}, u32[]{:S(2)}) collective-permute-start(bf16[66,1536]{1,0:T(8,128)(2,1)S(1)} %get-tuple-element.147.outgoing), channel_id=1, source_target_pairs={{544,512},{545,513},{546,514},{547,515},{548,516},{549,517},{550,5... | collective-permute-start | bytes 608264 | tf_op jit(solution)/shard_map/ppermute | solution.py:207
  347.5 41.3 %collective-permute-start.17 = (bf16[66,1536]{1,0:T(8,128)(2,1)S(1)}, bf16[66,1536]{1,0:T(8,128)(2,1)S(1)}, u32[]{:S(2)}, u32[]{:S(2)}) collective-permute-start(bf16[66,1536]{1,0:T(8,128)(2,1)S(1)} %get-tuple-element.147.outgoing), channel_id=1, source_target_pairs={{544,636},{545,637},{546,638},{547,639},{548,632},{549,633},{550,6... | collective-permute-start | bytes 608264 | tf_op jit(solution)/shard_map/ppermute | solution.py:207
  391.1 44.5 %collective-permute-start.20 = (bf16[66,1536]{1,0:T(8,128)(2,1)S(1)}, bf16[66,1536]{1,0:T(8,128)(2,1)S(1)}, u32[]{:S(2)}, u32[]{:S(2)}) collective-permute-start(bf16[66,1536]{1,0:T(8,128)(2,1)S(1)} %get-tuple-element.151.outgoing), channel_id=1, source_target_pairs={{608,576},{609,577},{610,578},{611,579},{612,580},{613,581},{614,5... | collective-permute-start | bytes 608264 | tf_op jit(solution)/shard_map/ppermute | solution.py:207
  391.7 45.5 %collective-permute-start.19 = (bf16[66,1536]{1,0:T(8,128)(2,1)S(1)}, bf16[66,1536]{1,0:T(8,128)(2,1)S(1)}, u32[]{:S(2)}, u32[]{:S(2)}) collective-permute-start(bf16[66,1536]{1,0:T(8,128)(2,1)S(1)} %get-tuple-element.151.outgoing), channel_id=1, source_target_pairs={{608,700},{609,701},{610,702},{611,703},{612,696},{613,697},{614,6... | collective-permute-start | bytes 608264 | tf_op jit(solution)/shard_map/ppermute | solution.py:207
  439.6 42.4 %collective-permute-start.22 = (bf16[66,1536]{1,0:T(8,128)(2,1)S(1)}, bf16[66,1536]{1,0:T(8,128)(2,1)S(1)}, u32[]{:S(2)}, u32[]{:S(2)}) collective-permute-start(bf16[66,1536]{1,0:T(8,128)(2,1)S(1)} %get-tuple-element.155.outgoing), channel_id=1, source_target_pairs={{672,640},{673,641},{674,642},{675,643},{676,644},{677,645},{678,6... | collective-permute-start | bytes 608264 | tf_op jit(solution)/shard_map/ppermute | solution.py:207
  440.3 43.4 %collective-permute-start.21 = (bf16[66,1536]{1,0:T(8,128)(2,1)S(1)}, bf16[66,1536]{1,0:T(8,128)(2,1)S(1)}, u32[]{:S(2)}, u32[]{:S(2)}) collective-permute-start(bf16[66,1536]{1,0:T(8,128)(2,1)S(1)} %get-tuple-element.155.outgoing), channel_id=1, source_target_pairs={{672,764},{673,765},{674,766},{675,767},{676,760},{677,761},{678,7... | collective-permute-start | bytes 608264 | tf_op jit(solution)/shard_map/ppermute | solution.py:207
  486.0 44.6 %collective-permute-start.24 = (bf16[66,1536]{1,0:T(8,128)(2,1)S(1)}, bf16[66,1536]{1,0:T(8,128)(2,1)S(1)}, u32[]{:S(2)}, u32[]{:S(2)}) collective-permute-start(bf16[66,1536]{1,0:T(8,128)(2,1)S(1)} %get-tuple-element.159.outgoing), channel_id=1, source_target_pairs={{736,704},{737,705},{738,706},{739,707},{740,708},{741,709},{742,7... | collective-permute-start | bytes 608264 | tf_op jit(solution)/shard_map/ppermute | solution.py:207
  486.7 45.6 %collective-permute-start.23 = (bf16[66,1536]{1,0:T(8,128)(2,1)S(1)}, bf16[66,1536]{1,0:T(8,128)(2,1)S(1)}, u32[]{:S(2)}, u32[]{:S(2)}) collective-permute-start(bf16[66,1536]{1,0:T(8,128)(2,1)S(1)} %get-tuple-element.159.outgoing), channel_id=1, source_target_pairs={{736,828},{737,829},{738,830},{739,831},{740,824},{741,825},{742,8... | collective-permute-start | bytes 608264 | tf_op jit(solution)/shard_map/ppermute | solution.py:207
  534.6 41.6 %collective-permute-start.26 = (bf16[66,1536]{1,0:T(8,128)(2,1)S(1)}, bf16[66,1536]{1,0:T(8,128)(2,1)S(1)}, u32[]{:S(2)}, u32[]{:S(2)}) collective-permute-start(bf16[66,1536]{1,0:T(8,128)(2,1)S(1)} %get-tuple-element.163.outgoing), channel_id=1, source_target_pairs={{800,768},{801,769},{802,770},{803,771},{804,772},{805,773},{806,7... | collective-permute-start | bytes 608264 | tf_op jit(solution)/shard_map/ppermute | solution.py:207
  535.3 42.6 %collective-permute-start.25 = (bf16[66,1536]{1,0:T(8,128)(2,1)S(1)}, bf16[66,1536]{1,0:T(8,128)(2,1)S(1)}, u32[]{:S(2)}, u32[]{:S(2)}) collective-permute-start(bf16[66,1536]{1,0:T(8,128)(2,1)S(1)} %get-tuple-element.163.outgoing), channel_id=1, source_target_pairs={{800,892},{801,893},{802,894},{803,895},{804,888},{805,889},{806,8... | collective-permute-start | bytes 608264 | tf_op jit(solution)/shard_map/ppermute | solution.py:207
  580.3 43.7 %collective-permute-start.28 = (bf16[66,1536]{1,0:T(8,128)(2,1)S(1)}, bf16[66,1536]{1,0:T(8,128)(2,1)S(1)}, u32[]{:S(2)}, u32[]{:S(2)}) collective-permute-start(bf16[66,1536]{1,0:T(8,128)(2,1)S(1)} %get-tuple-element.167.outgoing), channel_id=1, source_target_pairs={{864,832},{865,833},{866,834},{867,835},{868,836},{869,837},{870,8... | collective-permute-start | bytes 608264 | tf_op jit(solution)/shard_map/ppermute | solution.py:207
  580.9 44.8 %collective-permute-start.27 = (bf16[66,1536]{1,0:T(8,128)(2,1)S(1)}, bf16[66,1536]{1,0:T(8,128)(2,1)S(1)}, u32[]{:S(2)}, u32[]{:S(2)}) collective-permute-start(bf16[66,1536]{1,0:T(8,128)(2,1)S(1)} %get-tuple-element.167.outgoing), channel_id=1, source_target_pairs={{864,956},{865,957},{866,958},{867,959},{868,952},{869,953},{870,9... | collective-permute-start | bytes 608264 | tf_op jit(solution)/shard_map/ppermute | solution.py:207
  629.0 65.0 %collective-permute-start.30 = (bf16[66,1536]{1,0:T(8,128)(2,1)S(1)}, bf16[66,1536]{1,0:T(8,128)(2,1)}, u32[]{:S(2)}, u32[]{:S(2)}) collective-permute-start(bf16[66,1536]{1,0:T(8,128)(2,1)S(1)} %get-tuple-element.171.outgoing), channel_id=1, source_target_pairs={{928,896},{929,897},{930,898},{931,899},{932,900},{933,901},{934,9... | collective-permute-start | bytes 608264 | tf_op jit(solution)/shard_map/ppermute | solution.py:207
  693.3 76.2 %collective-permute-start.34 = (bf16[132,1536]{1,0:T(8,128)(2,1)}, bf16[132,1536]{1,0:T(8,128)(2,1)S(1)}, u32[]{:S(2)}, u32[]{:S(2)}) collective-permute-start(bf16[132,1536]{1,0:T(8,128)(2,1)} %reshape.24), channel_id=1, source_target_pairs={{960,988},{961,989},{962,990},{963,991},{964,984},{965,985},{966,9... | collective-permute-start | bytes 1216520 | tf_op jit(solution)/shard_map/ppermute | solution.py:207
  700.6 61.1 %collective-permute-start.32 = (bf16[66,1536]{1,0:T(8,128)(2,1)S(1)}, bf16[66,1536]{1,0:T(8,128)(2,1)S(1)}, u32[]{:S(2)}, u32[]{:S(2)}) collective-permute-start(bf16[66,1536]{1,0:T(8,128)(2,1)S(1)} %get-tuple-element.175.outgoing), channel_id=1, source_target_pairs={{992,960},{993,961},{994,962},{995,963},{996,964},{997,965},{998,9... | collective-permute-start | bytes 608264 | tf_op jit(solution)/shard_map/ppermute | solution.py:207
  781.8 51.5 %collective-permute-start.37 = (bf16[66,1536]{1,0:T(8,128)(2,1)S(1)}, bf16[66,1536]{1,0:T(8,128)(2,1)S(1)}, u32[]{:S(2)}, u32[]{:S(2)}) collective-permute-start(bf16[66,1536]{1,0:T(8,128)(2,1)S(1)} %get-tuple-element.187), channel_id=1, source_target_pairs={{896,860},{897,861},{898,862},{899,863},{900,856},{901,857},{902,8... | collective-permute-start | bytes 608264 | tf_op jit(solution)/shard_map/ppermute | solution.py:207
  868.1 158.5 %collective-permute-start.48 = (bf16[66,1536]{1,0:T(8,128)(2,1)S(1)}, bf16[66,1536]{1,0:T(8,128)(2,1)S(1)}, u32[]{:S(2)}, u32[]{:S(2)}) collective-permute-start(bf16[66,1536]{1,0:T(8,128)(2,1)S(1)} %get-tuple-element.205), channel_id=1, source_target_pairs={{384,348},{385,349},{386,350},{387,351},{388,344},{389,345},{390,3... | collective-permute-start | bytes 608264 | tf_op jit(solution)/shard_map/ppermute | solution.py:207
  868.9 152.9 %collective-permute-start.44 = (bf16[132,192]{1,0:T(8,128)(2,1)S(1)}, bf16[132,192]{1,0:T(8,128)(2,1)S(1)}, u32[]{:S(2)}, u32[]{:S(2)}) collective-permute-start(bf16[132,192]{1,0:T(8,128)(2,1)S(1)} %get-tuple-element.232), channel_id=1, source_target_pairs={{1,0},{2,1},{3,2},{0,3},{5,4},{6,5},{7,6},{4,7},{9,8},{10,9},{11,1... | collective-permute-start | bytes 152072 | tf_op jit(solution)/shard_map/ppermute | solution.py:287
  974.4 47.4 %collective-permute-start.45 = (bf16[132,192]{1,0:T(8,128)(2,1)S(1)}, bf16[132,192]{1,0:T(8,128)(2,1)S(1)}, u32[]{:S(2)}, u32[]{:S(2)}) collective-permute-start(bf16[132,192]{1,0:T(8,128)(2,1)S(1)} %get-tuple-element.231), channel_id=1, source_target_pairs={{2,0},{3,1},{0,2},{1,3},{6,4},{7,5},{4,6},{5,7},{10,8},{11,9},{8,1... | collective-permute-start | bytes 152072 | tf_op jit(solution)/shard_map/ppermute | solution.py:287
  1052.4 131.3 %collective-permute-start.62 = (bf16[264,1536]{1,0:T(8,128)(2,1)S(1)}, bf16[264,1536]{1,0:T(8,128)(2,1)S(1)}, u32[]{:S(2)}, u32[]{:S(2)}) collective-permute-start(bf16[264,1536]{1,0:T(8,128)(2,1)S(1)} %pad_maximum_fusion.1), channel_id=1, source_target_pairs={{0,32},{1,33},{2,34},{3,35},{4,36},{5,37},{6,38},{7,39},{8,40},{9,... | collective-permute-start | bytes 2433032 | tf_op jit(solution)/shard_map/ppermute | solution.py:207
  1195.2 48.7 %collective-permute-start.63 = (bf16[4,24,1536]{2,1,0:T(8,128)(2,1)S(1)}, bf16[4,24,1536]{2,1,0:T(8,128)(2,1)S(1)}, u32[]{:S(2)}, u32[]{:S(2)}) collective-permute-start(bf16[4,24,1536]{2,1,0:T(8,128)(2,1)S(1)} %dynamic-slice_convert_fusion), channel_id=1, source_target_pairs={{0,16},{1,17},{2,18},{3,19},{4,20},{5,21},{6,22},{7,23},{8,24},{9,... | collective-permute-start | bytes 884744 | tf_op jit(solution)/shard_map/ppermute | solution.py:379
  (52 other events, 537.8 us)

commit v2 on v1

--- a/solution.py
+++ b/solution.py
@@ -100,9 +100,7 @@
             kept[jnp.clip(chunk, 0, chunk_count - 1), :, part] = product
 
 
-def residual_kernel(
-    step, place, received, outgoing, zero_rows, second_rows, sides_in, residual, sides
-):
+def residual_kernel(step, place, received, zero_rows, second_rows, sides_in, residual, sides):
     del sides_in
     half, width = zero_rows.shape
     size = min(256, width)
@@ -122,11 +120,7 @@
 
     @pl.when((place[0] == 1) & in_chunks(chunk))
     def _():
-        sides[slot] = received[:, :half]
-
-    @pl.when((place[0] == 0) & in_chunks(chunk))
-    def _():
-        sides[slot] = outgoing[:, half:]
+        sides[slot] = received[...]
 
 
 def back_kernel(step, last_depth, has_arrived, has_own, has_slopes, *refs):
@@ -211,12 +205,47 @@
             step - chunk for chunk in range(chunk_count) if 0 <= step - chunk < block_count
         ]
 
-    last_base = section_count - 2
-    second_rows = move(
-        zero_rows, [(2 * block + 1, 2 * block) for block in range(block_count)], False
-    )
+    to_base = [(2 * block + 1, 2 * block) for block in range(block_count)]
+    to_control = [(2 * block, 2 * block + 1) for block in range(block_count)]
+
+    def forward_hops(step):
+        last = block_count + chunk_count - 2
+        if step < 3:
+            steps = range(3)
+        elif step > last - 3:
+            steps = range(last - 2, last + 1)
+        else:
+            steps = (step,)
+        return sorted(
+            {
+                (2 * block + 1 - lag, 2 * block + 3 - lag)
+                for each in steps
+                for lag in (0, 1)
+                for block in active_blocks(each - lag)
+                if block + 1 < block_count
+            }
+        )
+
+    def backward_hops(step):
+        last = block_count + chunk_count - 3
+        if step < 3:
+            steps = range(3)
+        elif step > last - 2:
+            steps = range(last - 1, last + 1)
+        else:
+            steps = (step,)
+        return sorted(
+            {
+                (2 * (block_count - 1 - back), 2 * (block_count - 2 - back))
+                for each in steps
+                for back in active_blocks(each)
+                if back + 1 < block_count
+            }
+        )
+
+    second_rows = move(zero_rows, to_base, False)
     upstream_rows = move(
-        upstream.reshape(all_rows, width), [(last_base, last_base)], True
+        upstream.reshape(all_rows, width), forward_hops(block_count), True
     ).reshape(chunk_count, rows, width)
 
     ordered = jnp.take(latents, batch_order, axis=0)
@@ -230,7 +259,7 @@
     arrived = None
     residual = jnp.zeros((rows, width), jnp.float32)
     products = jnp.zeros((chunk_count, rows, width), jnp.float32)
-    sides = jnp.zeros((chunk_count, rows, half), jnp.bfloat16)
+    sides = jnp.zeros((chunk_count, rows, width), jnp.bfloat16)
     for step in range(block_count + chunk_count):
         entering = ()
         if arrived is not None:
@@ -249,23 +278,16 @@
             {3 + len(entering): 1},
             (row_buffer,),
         )
-        hops = [
-            (2 * block + 1 - lag, 2 * block + 3 - lag)
-            for lag in (0, 1)
-            for block in active_blocks(step - lag)
-            if block + 1 < block_count
-        ]
-        if hops:
-            arrived = move(outgoing, hops, True)
-        shares = [(2 * block + 1, 2 * block) for block in active_blocks(step)]
-        if shares:
-            received = move(outgoing, shares, False)
+        if step < block_count + chunk_count - 1:
+            arrived = move(outgoing, forward_hops(step), True)
+        if step < block_count + chunk_count - 1:
+            received = move(outgoing, to_base, False)
             residual, sides = local_call(
                 functools.partial(residual_kernel, step),
-                (place, received, outgoing, zero_rows, second_rows, sides),
+                (place, received, zero_rows, second_rows, sides),
                 (shape_of(residual), shape_of(sides)),
                 256,
-                {5: 1},
+                {4: 1},
             )
 
     (slopes,) = local_call(
@@ -276,22 +298,20 @@
         {},
     )
 
-    def along_x(value, shift, section_pairs=None):
-        sections = range(section_count) if section_pairs is None else section_pairs
+    def along_x(value, shift):
         pairs = [
             (section * dp_count + z * x_size + (x + shift) % x_size, section * dp_count + z * x_size + x)
-            for section in sections
+            for section in range(0, section_count, 2)
             for z in range(z_size)
             for x in range(x_size)
         ]
         return lax.ppermute(value, both_axes, pairs)
 
-    base_sections = range(0, section_count, 2)
+    quarter = half // x_size
 
     def spread_side(side):
         source = lax.broadcasted_iota(jnp.int32, (half, half), 0)
         target = lax.broadcasted_iota(jnp.int32, (half, half), 1)
-        quarter = half // x_size
         piece = quarter // z_size
         shift = target // quarter
         within = target % quarter
@@ -301,18 +321,22 @@
             + within % piece
         )
         picks = (source == wanted).astype(jnp.bfloat16)
-        picked = jnp.dot(side, picks, preferred_element_type=jnp.float32).astype(jnp.bfloat16)
-        parts = [picked[:, shift * quarter : (shift + 1) * quarter] for shift in range(x_size)]
+        picked = [
+            jnp.dot(part, picks, preferred_element_type=jnp.float32).astype(jnp.bfloat16)
+            for part in (side[:, :half], side[:, half:])
+        ]
+        parts = [
+            jnp.concatenate(
+                [part[:, shift * quarter : (shift + 1) * quarter] for part in picked], axis=1
+            )
+            for shift in range(x_size)
+        ]
         return [parts[0]] + [along_x(parts[shift], shift) for shift in range(1, x_size)]
 
     def spread_grad(grad):
         return jnp.concatenate(
-            [grad] + [along_x(grad, shift, base_sections) for shift in range(1, x_size)], axis=0
-        )
-
-    def share_grad(gathered):
-        shared = move(gathered, [(2 * block, 2 * block + 1) for block in range(block_count)], False)
-        return jnp.where(is_base, gathered, shared)
+            [grad] + [along_x(grad, shift) for shift in range(1, x_size)], axis=0
+        )
 
     grads = jnp.zeros((chunk_count, rows, width), jnp.bfloat16)
     spread_sides = None
@@ -320,26 +344,21 @@
     for step in range(block_count + chunk_count - 1):
         if step == block_count // 2:
             sides, arrived = lax.optimization_barrier((sides, arrived))
-            spread = spread_side(sides.reshape(all_rows, half))
+            spread = spread_side(sides.reshape(all_rows, width))
         if step == block_count // 2 + 2:
-            spread, arrived = lax.optimization_barrier((spread, arrived))
             spread_sides = [
                 jnp.concatenate([part[chunk * rows : (chunk + 1) * rows] for part in spread])
                 for chunk in range(chunk_count)
             ]
+            spread_sides, arrived = lax.optimization_barrier((spread_sides, arrived))
         entering = ()
         if step > 0:
             entering += (arrived,)
         if step < chunk_count:
             entering += (upstream_rows[step],)
-        hops = [
-            (2 * (block_count - 1 - back), 2 * (block_count - 2 - back))
-            for back in active_blocks(step)
-            if back + 1 < block_count
-        ]
         done_chunk = step - (block_count - 1)
         grad_in = arrived
-        if hops:
+        if step < block_count + chunk_count - 2:
             outgoing, grads = local_call(
                 functools.partial(
                     back_kernel, step, block_count - 1, step > 0, step < chunk_count, True
@@ -350,7 +369,7 @@
                 {3 + len(entering): 1},
                 (row_buffer, row_buffer),
             )
-            arrived = move(outgoing, hops, True)
+            arrived = move(outgoing, backward_hops(step), True)
         if 0 <= done_chunk < chunk_count - 1:
             gathered = spread_grad(grads[done_chunk])
             gathered, arrived = lax.optimization_barrier((gathered, arrived))
@@ -359,14 +378,16 @@
         if done_chunk >= 0:
             grad_parts[done_chunk] = lax.dot_general(
                 spread_sides[done_chunk],
-                share_grad(gathered),
+                gathered,
                 (((0,), (0,)), ((), ())),
                 preferred_element_type=jnp.float32,
             )
 
-    partial_value = sum(grad_parts[1:], grad_parts[0]).reshape(
-        z_size, half // dp_count, width
-    )
+    both_values = sum(grad_parts[1:], grad_parts[0])
+    control_value = move(both_values[quarter:].astype(jnp.bfloat16), to_control, False)
+    partial_value = jnp.where(
+        is_base, both_values[:quarter], control_value.astype(jnp.float32)
+    ).reshape(z_size, half // dp_count, width)
     distance = z_size // 2
     while distance:
         upper = (z_place // distance) % 2

time: 1310 us -> 676 us (0.52)
  starting transfers between devices: 1070 us -> 125 us
  waiting for transfers between devices: 84.1 us -> 394 us
    ppermute x54 -> x53, starting transfers between devices: 854 us -> 113 us  [move(): return lax.ppermute(value, both_axes, pairs)]
    ppermute x54 -> x53, waiting for transfers between devices: 31.7 us -> 367 us  [move(): return lax.ppermute(value, both_axes, pairs)]
    ppermute x9, starting transfers between devices: 157 us -> 6.05 us  [along_x(): return lax.ppermute(value, both_axes, pairs)]
    ppermute x3, starting transfers between devices: 57.1 us -> 5.76 us  [body(): lax.ppermute(sent.astype(jnp.bfloat16), 'dp', pairs).astype(jnp.float32)]
    ppermute x3, waiting for transfers between devices: 47.6 us -> 27 us  [body(): lax.ppermute(sent.astype(jnp.bfloat16), 'dp', pairs).astype(jnp.float32)]
  transfers between devices with their start and end apart: 66 -> 65, of which waited for: 7 -> 21; matrix products, arithmetic and copies ran while one was open for 1% -> 1% of each run, Pallas kernels for 3% -> 6%
where the time goes in v2:
time: 676 us; the launch traced here: 672 us
  waiting for transfers between devices  394 us (58%)
  starting transfers between devices  125 us (18%)
  Pallas kernels  120 us (18%)
  local copies, waits for them, and re-layouts  22.9 us (3%)
    ppermute x53, waiting for transfers between devices, move(): return lax.ppermute(value, both_axes, pairs)  367 us
    pallas_call x52, Pallas kernels, local_call(): pl.pallas_call(kernel, out_shape=results, in_specs=[in_smem] + [in_vmem]...  120 us
    ppermute x53, starting transfers between devices, move(): return lax.ppermute(value, both_axes, pairs)  113 us
    ppermute x3, waiting for transfers between devices, body(): lax.ppermute(sent.astype(jnp.bfloat16), 'dp', pairs).astype(jnp.float32)  27 us
    unnamed x40, local copies, waits for them, and re-layouts  16.4 us
  transfers between devices with their start and end apart: 65, of which 21 were waited for; matrix products, arithmetic and copies ran while one was open for 1% of the time, Pallas kernels for 6%

profile of v2, /device:TPU:1, one launch (start us, length us, event | category | flops | bytes accessed | tf_op | source)
XLA Modules:
  0.0 672.2 jit_solution(7885446281975484657)
XLA Ops:
  0.0 17.6 %collective-permute-start.2 = (bf16[768,1536]{1,0:T(8,128)(2,1)}, bf16[768,1536]{1,0:T(8,128)(2,1)}, u32[]{:S(2)}, u32[]{:S(2)}) collective-permute-start(bf16[768,1536]{1,0:T(8,128)(2,1)} %bitcast.52), channel_id=1, source_target_pairs={{32,0},{33,1},{34,2},{35,3},{36,4},{37,5},{38,6},{39,7},{40,8},{41... | collective-permute-start | bytes 7077896 | tf_op jit(solution)/shard_map/ppermute | solution.py:201
  24.7 3.0 shard_map.64
  28.7 6.0 collective-permute-start
  40.7 11.5 %collective-permute-done.refs_1_ = bf16[66,1536]{1,0:T(8,128)(2,1)} collective-permute-done((bf16[66,1536]{1,0:T(8,128)(2,1)}, bf16[66,1536]{1,0:T(8,128)(2,1)}, u32[]{:S(2)}, u32[]{:S(2)}) %collective-permute-start) | collective-permute-done | bytes 202784 | tf_op jit(solution)/shard_map/ppermute | solution.py:201
  54.5 2.9 shard_map.66
  58.7 5.2 collective-permute-start.3
  65.7 11.3 %collective-permute-done.3.refs_1_ = bf16[66,1536]{1,0:T(8,128)(2,1)S(1)} collective-permute-done((bf16[66,1536]{1,0:T(8,128)(2,1)S(1)}, bf16[66,1536]{1,0:T(8,128)(2,1)S(1)}, u32[]{:S(2)}, u32[]{:S(2)}) %collective-permute-start.3) | collective-permute-done | bytes 202784 | tf_op jit(solution)/shard_map/ppermute | solution.py:201
  81.7 5.3 collective-permute-start.5
  88.7 8.5 %collective-permute-done.5.refs_1_ = bf16[66,1536]{1,0:T(8,128)(2,1)S(1)} collective-permute-done((bf16[66,1536]{1,0:T(8,128)(2,1)S(1)}, bf16[66,1536]{1,0:T(8,128)(2,1)S(1)}, u32[]{:S(2)}, u32[]{:S(2)}) %collective-permute-start.5) | collective-permute-done | bytes 202784 | tf_op jit(solution)/shard_map/ppermute | solution.py:201
  107.0 3.9 collective-permute-start.10
  116.0 3.9 collective-permute-start.12
  124.9 3.9 collective-permute-start.14
  133.9 3.9 collective-permute-start.16
  142.9 3.9 collective-permute-start.18
  151.9 3.9 collective-permute-start.20
  160.9 3.9 collective-permute-start.22
  169.9 3.9 collective-permute-start.24
  178.9 3.9 collective-permute-start.26
  187.8 3.9 collective-permute-start.28
  194.5 3.0 shard_map.92
  198.5 4.6 collective-permute-start.30
  222.5 3.9 collective-permute-start.33
  229.2 3.0 shard_map.98
  236.9 2.9 shard_map.101
  240.4 2.8 shard_map.102
  243.9 2.8 shard_map.103
  251.2 2.8 shard_map.105
  293.4 2.8 shard_map.115
  304.5 330.8 %collective-permute-done.61 = bf16[192,1536]{1,0:T(8,128)(2,1)} collective-permute-done((bf16[192,1536]{1,0:T(8,128)(2,1)S(1)}, bf16[192,1536]{1,0:T(8,128)(2,1)}, u32[]{:S(2)}, u32[]{:S(2)}) %collective-permute-start.61) | collective-permute-done | bytes 589856 | tf_op jit(solution)/shard_map/ppermute | solution.py:201
  639.4 18.0 %collective-permute-done.62 = bf16[4,24,1536]{2,1,0:T(8,128)(2,1)S(1)} collective-permute-done((bf16[4,24,1536]{2,1,0:T(8,128)(2,1)S(1)}, bf16[4,24,1536]{2,1,0:T(8,128)(2,1)S(1)}, u32[]{:S(2)}, u32[]{:S(2)}) %collective-permute-start.62) | collective-permute-done | bytes 294944 | tf_op jit(solution)/shard_map/ppermute | solution.py:400
  660.6 5.8 collective-permute-done.63
  668.4 3.2 collective-permute-done.64
  (240 shorter events, 173.9 us)
Async XLA Ops:
  0.0 37.9 %collective-permute-start.2 = (bf16[768,1536]{1,0:T(8,128)(2,1)}, bf16[768,1536]{1,0:T(8,128)(2,1)}, u32[]{:S(2)}, u32[]{:S(2)}) collective-permute-start(bf16[768,1536]{1,0:T(8,128)(2,1)} %bitcast.52), channel_id=1, source_target_pairs={{32,0},{33,1},{34,2},{35,3},{36,4},{37,5},{38,6},{39,7},{40,8},{41... | collective-permute-start | bytes 7077896 | tf_op jit(solution)/shard_map/ppermute | solution.py:201
  28.7 23.5 %collective-permute-start = (bf16[66,1536]{1,0:T(8,128)(2,1)}, bf16[66,1536]{1,0:T(8,128)(2,1)}, u32[]{:S(2)}, u32[]{:S(2)}) collective-permute-start(bf16[66,1536]{1,0:T(8,128)(2,1)} %get-tuple-element.114), channel_id=1, source_target_pairs={{0,92},{1,93},{2,94},{3,95},{4,88},{5,89},{6,90},{7,91},{8,84},{9,... | collective-permute-start | bytes 608264 | tf_op jit(solution)/shard_map/ppermute | solution.py:201
  57.4 6.5 collective-permute-start.4
  58.7 18.3 %collective-permute-start.3 = (bf16[66,1536]{1,0:T(8,128)(2,1)S(1)}, bf16[66,1536]{1,0:T(8,128)(2,1)S(1)}, u32[]{:S(2)}, u32[]{:S(2)}) collective-permute-start(bf16[66,1536]{1,0:T(8,128)(2,1)S(1)} %get-tuple-element.117), channel_id=1, source_target_pairs={{0,92},{1,93},{2,94},{3,95},{4,88},{5,89},{6,90},{7,91},{8,84},{9,... | collective-permute-start | bytes 608264 | tf_op jit(solution)/shard_map/ppermute | solution.py:201
  79.4 7.6 %collective-permute-start.6 = (bf16[66,1536]{1,0:T(8,128)(2,1)S(1)}, bf16[66,1536]{1,0:T(8,128)(2,1)S(1)}, u32[]{:S(2)}, u32[]{:S(2)}) collective-permute-start(bf16[66,1536]{1,0:T(8,128)(2,1)S(1)} %get-tuple-element.121), channel_id=1, source_target_pairs={{32,0},{33,1},{34,2},{35,3},{36,4},{37,5},{38,6},{39,7},{40,8},{41... | collective-permute-start | bytes 608264 | tf_op jit(solution)/shard_map/ppermute | solution.py:201
  81.7 15.6 %collective-permute-start.5 = (bf16[66,1536]{1,0:T(8,128)(2,1)S(1)}, bf16[66,1536]{1,0:T(8,128)(2,1)S(1)}, u32[]{:S(2)}, u32[]{:S(2)}) collective-permute-start(bf16[66,1536]{1,0:T(8,128)(2,1)S(1)} %get-tuple-element.121), channel_id=1, source_target_pairs={{0,92},{1,93},{2,94},{3,95},{4,88},{5,89},{6,90},{7,91},{8,84},{9,... | collective-permute-start | bytes 608264 | tf_op jit(solution)/shard_map/ppermute | solution.py:201
  99.6 3.4 collective-permute-start.8
  107.0 5.0 collective-permute-start.10
  116.0 5.0 collective-permute-start.12
  124.9 5.0 collective-permute-start.14
  128.8 2.8 collective-permute-start.13
  133.9 5.0 collective-permute-start.16
  142.9 5.0 collective-permute-start.18
  151.9 5.0 collective-permute-start.20
  160.9 5.0 collective-permute-start.22
  169.9 5.0 collective-permute-start.24
  178.9 5.0 collective-permute-start.26
  182.7 2.8 collective-permute-start.25
  187.8 5.0 collective-permute-start.28
  191.7 2.8 collective-permute-start.27
  198.5 7.8 %collective-permute-start.30 = (bf16[66,1536]{1,0:T(8,128)(2,1)}, bf16[66,1536]{1,0:T(8,128)(2,1)}, u32[]{:S(2)}, u32[]{:S(2)}) collective-permute-start(bf16[66,1536]{1,0:T(8,128)(2,1)} %get-tuple-element.169), channel_id=1, source_target_pairs={{32,0},{33,1},{34,2},{35,3},{36,4},{37,5},{38,6},{39,7},{40,8},{41... | collective-permute-start | bytes 608264 | tf_op jit(solution)/shard_map/ppermute | solution.py:201
  203.0 5.1 collective-permute-start.29
  205.5 21.5 %collective-permute-start.34 = (bf16[132,1536]{1,0:T(8,128)(2,1)}, bf16[132,1536]{1,0:T(8,128)(2,1)S(1)}, u32[]{:S(2)}, u32[]{:S(2)}) collective-permute-start(bf16[132,1536]{1,0:T(8,128)(2,1)} %reshape.24), channel_id=1, source_target_pairs={{768,860},{769,861},{770,862},{771,863},{772,856},{773,857},{774,8... | collective-permute-start | bytes 1216520 | tf_op jit(solution)/shard_map/ppermute | solution.py:201
  212.9 3.3 collective-permute-start.32
  222.5 5.0 collective-permute-start.33
  266.2 5.8 collective-permute-start.46
  266.9 5.1 collective-permute-start.45
  267.7 4.4 collective-permute-start.44
  303.1 332.1 %collective-permute-start.61 = (bf16[192,1536]{1,0:T(8,128)(2,1)S(1)}, bf16[192,1536]{1,0:T(8,128)(2,1)}, u32[]{:S(2)}, u32[]{:S(2)}) collective-permute-start(bf16[192,1536]{1,0:T(8,128)(2,1)S(1)} %slice.155), channel_id=1, source_target_pairs={{0,32},{1,33},{2,34},{3,35},{4,36},{5,37},{6,38},{7,39},{8,40},{9,... | collective-permute-start | bytes 1769480 | tf_op jit(solution)/shard_map/ppermute | solution.py:201
  637.5 20.0 %collective-permute-start.62 = (bf16[4,24,1536]{2,1,0:T(8,128)(2,1)S(1)}, bf16[4,24,1536]{2,1,0:T(8,128)(2,1)S(1)}, u32[]{:S(2)}, u32[]{:S(2)}) collective-permute-start(bf16[4,24,1536]{2,1,0:T(8,128)(2,1)S(1)} %dynamic-slice_convert_fusion), channel_id=1, source_target_pairs={{0,16},{1,17},{2,18},{3,19},{4,20},{5,21},{6,22},{7,23},{8,24},{9,... | collective-permute-start | bytes 884744 | tf_op jit(solution)/shard_map/ppermute | solution.py:400
  658.6 7.8 %collective-permute-start.63 = (bf16[2,24,1536]{2,1,0:T(8,128)(2,1)S(1)}, bf16[2,24,1536]{2,1,0:T(8,128)(2,1)S(1)}, u32[]{:S(2)}, u32[]{:S(2)}) collective-permute-start(bf16[2,24,1536]{2,1,0:T(8,128)(2,1)S(1)} %dynamic-slice_convert_fusion.1), channel_id=1, source_target_pairs={{0,8},{1,9},{2,10},{3,11},{4,12},{5,13},{6,14},{7,15},{8,0},{9,1},... | collective-permute-start | bytes 442376 | tf_op jit(solution)/shard_map/ppermute | solution.py:400
  666.4 5.1 collective-permute-start.64
  (53 other events, 212.2 us)

commit v3 on v2

--- a/solution.py
+++ b/solution.py
@@ -13,6 +13,7 @@
 chunk_count = 2
 x_size = 4
 both_axes = ("section", "dp")
+tile = 768
 
 
 def gelu_value(values):
@@ -85,7 +86,7 @@
     chunk = step - 1 - depth
     inputs = entry_rows(depth, 0, own, arrived, chosen)
     width = weight.shape[1]
-    size = min(256, width)
+    size = min(tile, width)
 
     @pl.loop(0, width // size)
     def _(index):
@@ -100,10 +101,12 @@
             kept[jnp.clip(chunk, 0, chunk_count - 1), :, part] = product
 
 
-def residual_kernel(step, place, received, zero_rows, second_rows, sides_in, residual, sides):
+def residual_kernel(
+    step, place, received, outgoing, zero_rows, second_rows, sides_in, residual, sides
+):
     del sides_in
     half, width = zero_rows.shape
-    size = min(256, width)
+    size = min(tile // 3, width)
     chunk = step - place[1]
     slot = jnp.clip(chunk, 0, chunk_count - 1)
 
@@ -118,46 +121,90 @@
                 received[:, half:], second_rows[:, part], preferred_element_type=jnp.float32
             )
 
-    @pl.when((place[0] == 1) & in_chunks(chunk))
-    def _():
-        sides[slot] = received[...]
-
-
-def back_kernel(step, last_depth, has_arrived, has_own, has_slopes, *refs):
+    @pl.when((place[0] == 0) & in_chunks(chunk))
+    def _():
+        sides[slot] = outgoing[...]
+
+
+def back_kernel(step, last_depth, has_arrived, has_own, *refs):
     refs = list(refs)
     place = refs.pop(0)
     arrived = refs.pop(0) if has_arrived else None
     own = refs.pop(0) if has_own else None
-    if has_slopes:
-        slopes, weight, kept_in, outgoing, kept, chosen, scaled = refs
-    else:
-        kept_in, kept, chosen = refs
+    slopes, weight, kept_in, outgoing, kept, chosen, scaled = refs
     del kept_in
     chunk = step - (last_depth - place[1])
     slot = jnp.clip(chunk, 0, chunk_count - 1)
     grad = entry_rows(place[1], last_depth, own, arrived, chosen)
-
-    if has_slopes:
-        width = weight.shape[1]
-        size = min(256, width)
-        scaled[...] = (grad[...].astype(jnp.float32) * slopes[slot]).astype(jnp.bfloat16)
-
+    width = weight.shape[1]
+    size = min(tile, width)
+    scaled[...] = (grad[...].astype(jnp.float32) * slopes[slot]).astype(jnp.bfloat16)
+
+    @pl.loop(0, width // size)
+    def _(index):
+        part = columns_of(index, size)
+        back_term = lax.dot_general(
+            scaled[...],
+            weight[part, :],
+            (((1,), (1,)), ((), ())),
+            preferred_element_type=jnp.float32,
+        )
+        outgoing[:, part] = (grad[:, part].astype(jnp.float32) + back_term).astype(jnp.bfloat16)
+
+    @pl.when(in_chunks(chunk))
+    def _():
+        kept[slot] = grad[...]
+
+
+def spread_kernel(place, sides, picks, *parts):
+    half = picks.shape[1]
+
+    @pl.when(place[0] == 0)
+    def _():
+        for shift, part in enumerate(parts):
+            for chunk in range(chunk_count):
+                for second in range(2):
+                    part[chunk, second] = jnp.dot(
+                        sides[chunk, :, second * half : (second + 1) * half],
+                        picks[shift],
+                        preferred_element_type=jnp.float32,
+                    ).astype(jnp.bfloat16)
+
+
+def finish_kernel(place, arrived, shared, kept, grads):
+    @pl.when(place[1] == 0)
+    def _():
+        for chunk in range(chunk_count - 1):
+            grads[chunk] = kept[chunk]
+        grads[chunk_count - 1] = arrived[...]
+
+    @pl.when(place[1] != 0)
+    def _():
+        grads[...] = shared[...]
+
+
+def reduce_kernel(place, *refs):
+    parts, grads, (second_value, first_value) = refs[:x_size], refs[x_size : 2 * x_size], refs[-2:]
+    width = first_value.shape[1]
+    size = min(512, width)
+
+    @pl.when(place[0] == 0)
+    def _():
         @pl.loop(0, width // size)
         def _(index):
-            part = columns_of(index, size)
-            back_term = lax.dot_general(
-                scaled[...],
-                weight[part, :],
-                (((1,), (1,)), ((), ())),
-                preferred_element_type=jnp.float32,
-            )
-            outgoing[:, part] = (grad[:, part].astype(jnp.float32) + back_term).astype(
-                jnp.bfloat16
-            )
-
-    @pl.when(in_chunks(chunk))
-    def _():
-        kept[slot] = grad[...]
+            columns = columns_of(index, size)
+            for second, target in enumerate((first_value, second_value)):
+                total = None
+                for part, grad in zip(parts, grads):
+                    for chunk in range(chunk_count):
+                        term = lax.dot_general(
+                            part[chunk, second],
+                            grad[chunk, :, columns],
+                            (((0,), (0,)), ((), ())),
+                            preferred_element_type=jnp.float32,
+                        )
+                        total = term if total is None else total + term
+                target[:, columns] = total.astype(target.dtype)
 
 
 def slope_kernel(products, slopes):
@@ -236,7 +283,10 @@
             steps = (step,)
         return sorted(
             {
-                (2 * (block_count - 1 - back), 2 * (block_count - 2 - back))
+                (
+                    2 * (block_count - 1 - back),
+                    max(1, 2 * (block_count - 2 - back)),
+                )
                 for each in steps
                 for back in active_blocks(each)
                 if back + 1 < block_count
@@ -244,14 +294,28 @@
         )
 
     second_rows = move(zero_rows, to_base, False)
-    upstream_rows = move(
-        upstream.reshape(all_rows, width), forward_hops(block_count), True
-    ).reshape(chunk_count, rows, width)
-
     ordered = jnp.take(latents, batch_order, axis=0)
     hinted = jnp.take(control_hint, batch_order, axis=0)
     started = (ordered.astype(jnp.float32) + hinted.astype(jnp.float32)).astype(jnp.bfloat16)
     first_rows = jnp.where(is_base, ordered, started).reshape(chunk_count, rows, width)
+    own_upstream = upstream.reshape(chunk_count, rows, width)
+    first_rows = [first_rows[chunk] for chunk in range(chunk_count)]
+    own_upstream = [own_upstream[chunk] for chunk in range(chunk_count)]
+    quarter = half // x_size
+    pick_shape = (x_size, half, quarter)
+    piece = quarter // z_size
+    within = lax.broadcasted_iota(jnp.int32, pick_shape, 2)
+    order = within // piece
+    z_target = jnp.zeros_like(order)
+    distance = 1
+    while distance < z_size:
+        z_target = z_target + (order // (z_size // (2 * distance))) % 2 * distance
+        distance *= 2
+    x_target = (x_place - lax.broadcasted_iota(jnp.int32, pick_shape, 0)) % x_size
+    wanted = (z_target * x_size + x_target) * piece + within % piece
+    picks = (lax.broadcasted_iota(jnp.int32, pick_shape, 1) == wanted).astype(jnp.bfloat16)
+    first_rows, own_upstream, picks = lax.optimization_barrier((first_rows, own_upstream, picks))
+    upstream_rows = [move(part, forward_hops(block_count), True) for part in own_upstream]
 
     place = jnp.stack([is_base.astype(jnp.int32), depth])
     row_buffer = pltpu.VMEM((rows, width), jnp.bfloat16)
@@ -262,6 +326,8 @@
     sides = jnp.zeros((chunk_count, rows, width), jnp.bfloat16)
     for step in range(block_count + chunk_count):
         entering = ()
+        if step == 4:
+            upstream_rows, arrived = lax.optimization_barrier((upstream_rows, arrived))
         if arrived is not None:
             entering += (arrived,)
         if step <= chunk_count:
@@ -284,10 +350,10 @@
             received = move(outgoing, to_base, False)
             residual, sides = local_call(
                 functools.partial(residual_kernel, step),
-                (place, received, zero_rows, second_rows, sides),
+                (place, received, outgoing, zero_rows, second_rows, sides),
                 (shape_of(residual), shape_of(sides)),
                 256,
-                {4: 1},
+                {5: 1},
             )
 
     (slopes,) = local_call(
@@ -301,67 +367,33 @@
     def along_x(value, shift):
         pairs = [
             (section * dp_count + z * x_size + (x + shift) % x_size, section * dp_count + z * x_size + x)
-            for section in range(0, section_count, 2)
+            for section in range(1, section_count, 2)
             for z in range(z_size)
             for x in range(x_size)
         ]
         return lax.ppermute(value, both_axes, pairs)
 
-    quarter = half // x_size
-
     def spread_side(side):
-        source = lax.broadcasted_iota(jnp.int32, (half, half), 0)
-        target = lax.broadcasted_iota(jnp.int32, (half, half), 1)
-        piece = quarter // z_size
-        shift = target // quarter
-        within = target % quarter
-        wanted = (
-            (within // piece) * piece * x_size
-            + ((x_place - shift) % x_size) * piece
-            + within % piece
-        )
-        picks = (source == wanted).astype(jnp.bfloat16)
-        picked = [
-            jnp.dot(part, picks, preferred_element_type=jnp.float32).astype(jnp.bfloat16)
-            for part in (side[:, :half], side[:, half:])
-        ]
-        parts = [
-            jnp.concatenate(
-                [part[:, shift * quarter : (shift + 1) * quarter] for part in picked], axis=1
-            )
-            for shift in range(x_size)
-        ]
+        part_shape = jax.ShapeDtypeStruct((chunk_count, 2, rows, quarter), jnp.bfloat16)
+        parts = local_call(spread_kernel, (place, side, picks), (part_shape,) * x_size, 256, {})
         return [parts[0]] + [along_x(parts[shift], shift) for shift in range(1, x_size)]
 
-    def spread_grad(grad):
-        return jnp.concatenate(
-            [grad] + [along_x(grad, shift) for shift in range(1, x_size)], axis=0
-        )
-
     grads = jnp.zeros((chunk_count, rows, width), jnp.bfloat16)
-    spread_sides = None
-    grad_parts = [None] * chunk_count
+    spread = joined = None
     for step in range(block_count + chunk_count - 1):
         if step == block_count // 2:
-            sides, arrived = lax.optimization_barrier((sides, arrived))
-            spread = spread_side(sides.reshape(all_rows, width))
-        if step == block_count // 2 + 2:
-            spread_sides = [
-                jnp.concatenate([part[chunk * rows : (chunk + 1) * rows] for part in spread])
-                for chunk in range(chunk_count)
-            ]
-            spread_sides, arrived = lax.optimization_barrier((spread_sides, arrived))
+            joined = sides
+        if step == block_count // 2 + 1:
+            spread, arrived = lax.optimization_barrier((spread, arrived))
         entering = ()
         if step > 0:
             entering += (arrived,)
         if step < chunk_count:
             entering += (upstream_rows[step],)
-        done_chunk = step - (block_count - 1)
-        grad_in = arrived
         if step < block_count + chunk_count - 2:
             outgoing, grads = local_call(
                 functools.partial(
-                    back_kernel, step, block_count - 1, step > 0, step < chunk_count, True
+                    back_kernel, step, block_count - 1, step > 0, step < chunk_count
                 ),
                 (place,) + entering + (slopes, weight, grads),
                 (row_shape, shape_of(grads)),
@@ -370,29 +402,38 @@
                 (row_buffer, row_buffer),
             )
             arrived = move(outgoing, backward_hops(step), True)
-        if 0 <= done_chunk < chunk_count - 1:
-            gathered = spread_grad(grads[done_chunk])
-            gathered, arrived = lax.optimization_barrier((gathered, arrived))
-        elif done_chunk >= 0:
-            gathered = spread_grad(jnp.where(depth == 0, grad_in, grads[done_chunk]))
-        if done_chunk >= 0:
-            grad_parts[done_chunk] = lax.dot_general(
-                spread_sides[done_chunk],
-                gathered,
-                (((0,), (0,)), ((), ())),
-                preferred_element_type=jnp.float32,
-            )
-
-    both_values = sum(grad_parts[1:], grad_parts[0])
-    control_value = move(both_values[quarter:].astype(jnp.bfloat16), to_control, False)
-    partial_value = jnp.where(
-        is_base, both_values[:quarter], control_value.astype(jnp.float32)
-    ).reshape(z_size, half // dp_count, width)
-    distance = z_size // 2
-    while distance:
+            if step == block_count // 2:
+                joined, outgoing = lax.optimization_barrier((joined, outgoing))
+                spread = spread_side(joined)
+
+    (grads,) = local_call(
+        finish_kernel,
+        (place, arrived, move(grads, to_control, False), grads),
+        (shape_of(grads),),
+        256,
+        {},
+    )
+    value_shape = (quarter, width)
+    control_value, base_value = local_call(
+        reduce_kernel,
+        (place, *spread, grads) + tuple(along_x(grads, shift) for shift in range(1, x_size)),
+        (
+            jax.ShapeDtypeStruct(value_shape, jnp.float32),
+            jax.ShapeDtypeStruct(value_shape, jnp.bfloat16),
+        ),
+        256,
+        {},
+    )
+    base_value = move(base_value, to_base, False)
+    partial_value = jnp.where(is_base, base_value.astype(jnp.float32), control_value).reshape(
+        z_size, half // dp_count, width
+    )
+    distance = 1
+    while distance < z_size:
         upper = (z_place // distance) % 2
-        kept = lax.dynamic_slice_in_dim(partial_value, upper * distance, distance, 0)
-        sent = lax.dynamic_slice_in_dim(partial_value, (1 - upper) * distance, distance, 0)
+        kept_size = partial_value.shape[0] // 2
+        kept = lax.dynamic_slice_in_dim(partial_value, upper * kept_size, kept_size, 0)
+        sent = lax.dynamic_slice_in_dim(partial_value, (1 - upper) * kept_size, kept_size, 0)
         pairs = [
             (place, ((place // x_size) ^ distance) * x_size + place % x_size)
             for place in range(dp_count)
@@ -400,7 +441,7 @@
         partial_value = kept + lax.ppermute(sent.astype(jnp.bfloat16), "dp", pairs).astype(
             jnp.float32
         )
-        distance //= 2
+        distance *= 2
     grad_scale = 1.0 / math.sqrt(all_rows * dp_count)
     return partial_value * grad_scale
 

time: 676 us -> 625 us (0.925)
  Pallas kernels: 120 us -> 84.9 us
  waiting for transfers between devices: 394 us -> 376 us
  starting transfers between devices: 125 us -> 142 us
  local copies, waits for them, and re-layouts: 22.9 us -> 13.9 us
    pallas_call x52 -> x55, Pallas kernels: 120 us -> 84.9 us  [local_call(): pl.pallas_call(kernel, out_shape=results, in_specs=[in_smem] + [in_vmem]...]
    ppermute x53 -> x55, waiting for transfers between devices: 367 us -> 334 us  [move(): return lax.ppermute(value, both_axes, pairs)]
    ppermute x9 -> x6, waiting for transfers between devices: 0.02 us -> 14.9 us  [along_x(): return lax.ppermute(value, both_axes, pairs)]
    ppermute x9 -> x6, starting transfers between devices: 6.05 us -> 18.6 us  [along_x(): return lax.ppermute(value, both_axes, pairs)]
    unnamed x40 -> x16, local copies, waits for them, and re-layouts: 16.4 us -> 4.69 us
    ppermute x53 -> x55, starting transfers between devices: 113 us -> 117 us  [move(): return lax.ppermute(value, both_axes, pairs)]
  transfers between devices with their start and end apart: 65 -> 64, of which waited for: 21 -> 29; matrix products, arithmetic and copies ran while one was open for 1% -> 2% of each run, Pallas kernels for 6% -> 2%
where the time goes in v3:
time: 625 us; the launch traced here: 623 us
  waiting for transfers between devices  376 us (60%)
  starting transfers between devices  142 us (23%)
  Pallas kernels  84.9 us (14%)
  local copies, waits for them, and re-layouts  13.9 us (2%)
    ppermute x55, waiting for transfers between devices, move(): return lax.ppermute(value, both_axes, pairs)  334 us
    ppermute x55, starting transfers between devices, move(): return lax.ppermute(value, both_axes, pairs)  117 us
    pallas_call x55, Pallas kernels, local_call(): pl.pallas_call(kernel, out_shape=results, in_specs=[in_smem] + [in_vmem]...  84.9 us
    ppermute x3, waiting for transfers between devices, body(): lax.ppermute(sent.astype(jnp.bfloat16), 'dp', pairs).astype(jnp.float32)  27.3 us
    ppermute x6, starting transfers between devices, along_x(): return lax.ppermute(value, both_axes, pairs)  18.6 us
    ppermute x6, waiting for transfers between devices, along_x(): return lax.ppermute(value, both_axes, pairs)  14.9 us
  transfers between devices with their start and end apart: 64, of which 29 were waited for; matrix products, arithmetic and copies ran while one was open for 2% of the time, Pallas kernels for 2%

profile of v3, /device:TPU:1, one launch (start us, length us, event | category | flops | bytes accessed | tf_op | source)
XLA Modules:
  0.0 623.3 jit_solution(3686760800418827117)
XLA Ops:
  0.0 16.3 %collective-permute-start.4 = (bf16[768,1536]{1,0:T(8,128)(2,1)}, bf16[768,1536]{1,0:T(8,128)(2,1)S(1)}, u32[]{:S(2)}, u32[]{:S(2)}) collective-permute-start(bf16[768,1536]{1,0:T(8,128)(2,1)} %bitcast.39), channel_id=1, source_target_pairs={{32,0},{33,1},{34,2},{35,3},{36,4},{37,5},{38,6},{39,7},{40,8},{41... | collective-permute-start | bytes 7077896 | tf_op jit(solution)/shard_map/ppermute | solution.py:248
  34.0 5.3 collective-permute-start.2
  42.4 16.0 %collective-permute-done.2.refs_1_ = bf16[66,1536]{1,0:T(8,128)(2,1)S(1)} collective-permute-done((bf16[66,1536]{1,0:T(8,128)(2,1)S(1)}, bf16[66,1536]{1,0:T(8,128)(2,1)S(1)}, u32[]{:S(2)}, u32[]{:S(2)}) %collective-permute-start.2) | collective-permute-done | bytes 202784 | tf_op jit(solution)/shard_map/ppermute | solution.py:248
  64.9 5.3 collective-permute-start.5
  70.7 12.8 %collective-permute-done.5.refs_1_ = bf16[66,1536]{1,0:T(8,128)(2,1)S(1)} collective-permute-done((bf16[66,1536]{1,0:T(8,128)(2,1)S(1)}, bf16[66,1536]{1,0:T(8,128)(2,1)S(1)}, u32[]{:S(2)}, u32[]{:S(2)}) %collective-permute-start.5) | collective-permute-done | bytes 202784 | tf_op jit(solution)/shard_map/ppermute | solution.py:248
  87.7 5.3 collective-permute-start.7
  95.0 8.5 %collective-permute-done.7.refs_1_ = bf16[66,1536]{1,0:T(8,128)(2,1)S(1)} collective-permute-done((bf16[66,1536]{1,0:T(8,128)(2,1)S(1)}, bf16[66,1536]{1,0:T(8,128)(2,1)S(1)}, u32[]{:S(2)}, u32[]{:S(2)}) %collective-permute-start.7) | collective-permute-done | bytes 202784 | tf_op jit(solution)/shard_map/ppermute | solution.py:248
  111.6 3.9 collective-permute-start.12
  118.9 3.9 collective-permute-start.14
  126.1 3.9 collective-permute-start.16
  133.4 3.9 collective-permute-start.18
  140.7 3.9 collective-permute-start.20
  148.0 3.9 collective-permute-start.22
  155.3 3.9 collective-permute-start.24
  162.5 3.9 collective-permute-start.26
  169.8 3.9 collective-permute-start.28
  177.3 3.9 collective-permute-start.30
  184.6 3.9 collective-permute-start.32
  191.8 3.9 collective-permute-start.34
  199.1 3.9 collective-permute-start.35
  236.8 4.4 collective-permute-start.45
  243.7 2.5 collective-permute-start.47
  269.2 276.2 %collective-permute-done.54.refs_1_ = bf16[66,1536]{1,0:T(8,128)(2,1)S(1)} collective-permute-done((bf16[66,1536]{1,0:T(8,128)(2,1)S(1)}, bf16[66,1536]{1,0:T(8,128)(2,1)S(1)}, u32[]{:S(2)}, u32[]{:S(2)}) %collective-permute-start.54) | collective-permute-done | bytes 202784 | tf_op jit(solution)/shard_map/ppermute | solution.py:248
  550.3 11.4 %collective-permute-done.55.arrived = bf16[66,1536]{1,0:T(8,128)(2,1)S(1)} collective-permute-done((bf16[66,1536]{1,0:T(8,128)(2,1)S(1)}, bf16[66,1536]{1,0:T(8,128)(2,1)S(1)}, u32[]{:S(2)}, u32[]{:S(2)}) %collective-permute-start.55) | collective-permute-done | bytes 202784 | tf_op jit(solution)/shard_map/ppermute | solution.py:248
  562.2 4.4 collective-permute-start.57
  571.6 5.0 collective-permute-done.57.refs_5_
  577.3 4.6 collective-permute-done.59.refs_7_
  581.9 3.5 shard_map.118
  590.5 8.1 %collective-permute-done.61 = bf16[4,24,1536]{2,1,0:T(8,128)(2,1)S(1)} collective-permute-done((bf16[4,24,1536]{2,1,0:T(8,128)(2,1)S(1)}, bf16[4,24,1536]{2,1,0:T(8,128)(2,1)S(1)}, u32[]{:S(2)}, u32[]{:S(2)}) %collective-permute-start.61) | collective-permute-done | bytes 294944 | tf_op jit(solution)/shard_map/ppermute | solution.py:441
  600.7 9.7 %collective-permute-done.62 = bf16[2,24,1536]{2,1,0:T(8,128)(2,1)S(1)} collective-permute-done((bf16[2,24,1536]{2,1,0:T(8,128)(2,1)S(1)}, bf16[2,24,1536]{2,1,0:T(8,128)(2,1)S(1)}, u32[]{:S(2)}, u32[]{:S(2)}) %collective-permute-start.62) | collective-permute-done | bytes 147488 | tf_op jit(solution)/shard_map/ppermute | solution.py:441
  610.5 2.7 collective-permute-start.63
  613.2 9.5 %collective-permute-done.63 = bf16[1,24,1536]{2,1,0:T(8,128)(2,1)S(1)} collective-permute-done((bf16[1,24,1536]{2,1,0:T(8,128)(2,1)S(1)}, bf16[1,24,1536]{2,1,0:T(8,128)(2,1)S(1)}, u32[]{:S(2)}, u32[]{:S(2)}) %collective-permute-start.63) | collective-permute-done | bytes 73760 | tf_op jit(solution)/shard_map/ppermute | solution.py:441
  (198 shorter events, 159.7 us)
Async XLA Ops:
  0.0 41.8 %collective-permute-start.4 = (bf16[768,1536]{1,0:T(8,128)(2,1)}, bf16[768,1536]{1,0:T(8,128)(2,1)S(1)}, u32[]{:S(2)}, u32[]{:S(2)}) collective-permute-start(bf16[768,1536]{1,0:T(8,128)(2,1)} %bitcast.39), channel_id=1, source_target_pairs={{32,0},{33,1},{34,2},{35,3},{36,4},{37,5},{38,6},{39,7},{40,8},{41... | collective-permute-start | bytes 7077896 | tf_op jit(solution)/shard_map/ppermute | solution.py:248
  34.0 24.4 %collective-permute-start.2 = (bf16[66,1536]{1,0:T(8,128)(2,1)S(1)}, bf16[66,1536]{1,0:T(8,128)(2,1)S(1)}, u32[]{:S(2)}, u32[]{:S(2)}) collective-permute-start(bf16[66,1536]{1,0:T(8,128)(2,1)S(1)} %get-tuple-element.130.outgoing), channel_id=1, source_target_pairs={{0,92},{1,93},{2,94},{3,95},{4,88},{5,89},{6,90},{7,91},{8,84},{9,... | collective-permute-start | bytes 608264 | tf_op jit(solution)/shard_map/ppermute | solution.py:248
  62.6 7.6 %collective-permute-start.6 = (bf16[66,1536]{1,0:T(8,128)(2,1)S(1)}, bf16[66,1536]{1,0:T(8,128)(2,1)S(1)}, u32[]{:S(2)}, u32[]{:S(2)}) collective-permute-start(bf16[66,1536]{1,0:T(8,128)(2,1)S(1)} %get-tuple-element.134.outgoing), channel_id=1, source_target_pairs={{32,0},{33,1},{34,2},{35,3},{36,4},{37,5},{38,6},{39,7},{40,8},{41... | collective-permute-start | bytes 608264 | tf_op jit(solution)/shard_map/ppermute | solution.py:248
  64.9 18.7 %collective-permute-start.5 = (bf16[66,1536]{1,0:T(8,128)(2,1)S(1)}, bf16[66,1536]{1,0:T(8,128)(2,1)S(1)}, u32[]{:S(2)}, u32[]{:S(2)}) collective-permute-start(bf16[66,1536]{1,0:T(8,128)(2,1)S(1)} %get-tuple-element.134.outgoing), channel_id=1, source_target_pairs={{0,92},{1,93},{2,94},{3,95},{4,88},{5,89},{6,90},{7,91},{8,84},{9,... | collective-permute-start | bytes 608264 | tf_op jit(solution)/shard_map/ppermute | solution.py:248
  85.4 9.0 %collective-permute-start.8 = (bf16[66,1536]{1,0:T(8,128)(2,1)S(1)}, bf16[66,1536]{1,0:T(8,128)(2,1)S(1)}, u32[]{:S(2)}, u32[]{:S(2)}) collective-permute-start(bf16[66,1536]{1,0:T(8,128)(2,1)S(1)} %get-tuple-element.138.outgoing), channel_id=1, source_target_pairs={{32,0},{33,1},{34,2},{35,3},{36,4},{37,5},{38,6},{39,7},{40,8},{41... | collective-permute-start | bytes 608264 | tf_op jit(solution)/shard_map/ppermute | solution.py:248
  87.7 15.8 %collective-permute-start.7 = (bf16[66,1536]{1,0:T(8,128)(2,1)S(1)}, bf16[66,1536]{1,0:T(8,128)(2,1)S(1)}, u32[]{:S(2)}, u32[]{:S(2)}) collective-permute-start(bf16[66,1536]{1,0:T(8,128)(2,1)S(1)} %get-tuple-element.138.outgoing), channel_id=1, source_target_pairs={{0,92},{1,93},{2,94},{3,95},{4,88},{5,89},{6,90},{7,91},{8,84},{9,... | collective-permute-start | bytes 608264 | tf_op jit(solution)/shard_map/ppermute | solution.py:248
  93.0 15.2 %collective-permute-start = (bf16[66,1536]{1,0:T(8,128)(2,1)S(1)}, bf16[66,1536]{1,0:T(8,128)(2,1)S(1)}, u32[]{:S(2)}, u32[]{:S(2)}) collective-permute-start(bf16[66,1536]{1,0:T(8,128)(2,1)S(1)} %copy-done.7), channel_id=1, source_target_pairs={{768,860},{769,861},{770,862},{771,863},{772,856},{773,857},{774,8... | collective-permute-start | bytes 608264 | tf_op jit(solution)/shard_map/ppermute | solution.py:248
  93.7 14.5 %collective-permute-start.1 = (bf16[66,1536]{1,0:T(8,128)(2,1)S(1)}, bf16[66,1536]{1,0:T(8,128)(2,1)S(1)}, u32[]{:S(2)}, u32[]{:S(2)}) collective-permute-start(bf16[66,1536]{1,0:T(8,128)(2,1)S(1)} %copy-done.6), channel_id=1, source_target_pairs={{768,860},{769,861},{770,862},{771,863},{772,856},{773,857},{774,8... | collective-permute-start | bytes 608264 | tf_op jit(solution)/shard_map/ppermute | solution.py:248
  111.6 5.0 collective-permute-start.12
  118.9 5.0 collective-permute-start.14
  126.1 5.0 collective-permute-start.16
  133.4 5.0 collective-permute-start.18
  140.7 5.0 collective-permute-start.20
  148.0 5.0 collective-permute-start.22
  162.5 5.0 collective-permute-start.26
  177.3 5.0 collective-permute-start.30
  184.6 5.0 collective-permute-start.32
  191.8 5.0 collective-permute-start.34
  199.1 5.0 collective-permute-start.35
  234.4 16.4 %collective-permute-start.48 = (bf16[66,1536]{1,0:T(8,128)(2,1)S(1)}, bf16[66,1536]{1,0:T(8,128)(2,1)S(1)}, u32[]{:S(2)}, u32[]{:S(2)}) collective-permute-start(bf16[66,1536]{1,0:T(8,128)(2,1)S(1)} %get-tuple-element.219), channel_id=1, source_target_pairs={{448,412},{449,413},{450,414},{451,415},{452,408},{453,409},{454,4... | collective-permute-start | bytes 608264 | tf_op jit(solution)/shard_map/ppermute | solution.py:248
  236.8 9.3 %collective-permute-start.45 = (bf16[2,2,66,192]{3,2,1,0:T(8,128)(2,1)S(1)}, bf16[2,2,66,192]{3,2,1,0:T(8,128)(2,1)S(1)}, u32[]{:S(2)}, u32[]{:S(2)}) collective-permute-start(bf16[2,2,66,192]{3,2,1,0:T(8,128)(2,1)S(1)} %get-tuple-element.223), channel_id=1, source_target_pairs={{33,32},{34,33},{35,34},{32,35},{37,36},{38,37},{39,38},{36,39},{4... | collective-permute-start | bytes 304136 | tf_op jit(solution)/shard_map/ppermute | solution.py:374
  241.2 7.4 %collective-permute-start.46 = (bf16[2,2,66,192]{3,2,1,0:T(8,128)(2,1)S(1)}, bf16[2,2,66,192]{3,2,1,0:T(8,128)(2,1)S(1)}, u32[]{:S(2)}, u32[]{:S(2)}) collective-permute-start(bf16[2,2,66,192]{3,2,1,0:T(8,128)(2,1)S(1)} %get-tuple-element.224), channel_id=1, source_target_pairs={{34,32},{35,33},{32,34},{33,35},{38,36},{39,37},{36,38},{37,39},{4... | collective-permute-start | bytes 304136 | tf_op jit(solution)/shard_map/ppermute | solution.py:374
  243.7 7.1 %collective-permute-start.47 = (bf16[2,2,66,192]{3,2,1,0:T(8,128)(2,1)S(1)}, bf16[2,2,66,192]{3,2,1,0:T(8,128)(2,1)S(1)}, u32[]{:S(2)}, u32[]{:S(2)}) collective-permute-start(bf16[2,2,66,192]{3,2,1,0:T(8,128)(2,1)S(1)} %get-tuple-element.225), channel_id=1, source_target_pairs={{35,32},{32,33},{33,34},{34,35},{39,36},{36,37},{37,38},{38,39},{4... | collective-permute-start | bytes 304136 | tf_op jit(solution)/shard_map/ppermute | solution.py:374
  267.9 277.5 %collective-permute-start.54 = (bf16[66,1536]{1,0:T(8,128)(2,1)S(1)}, bf16[66,1536]{1,0:T(8,128)(2,1)S(1)}, u32[]{:S(2)}, u32[]{:S(2)}) collective-permute-start(bf16[66,1536]{1,0:T(8,128)(2,1)S(1)} %get-tuple-element.242), channel_id=1, source_target_pairs={{64,60},{65,61},{66,62},{67,63},{68,56},{69,57},{70,58},{71,59},{7... | collective-permute-start | bytes 608264 | tf_op jit(solution)/shard_map/ppermute | solution.py:248
  547.7 14.0 %collective-permute-start.56 = (bf16[2,66,1536]{2,1,0:T(8,128)(2,1)S(1)}, bf16[2,66,1536]{2,1,0:T(8,128)(2,1)S(1)}, u32[]{:S(2)}, u32[]{:S(2)}) collective-permute-start(bf16[2,66,1536]{2,1,0:T(8,128)(2,1)S(1)} %get-tuple-element.245.kept), channel_id=1, source_target_pairs={{0,32},{1,33},{2,34},{3,35},{4,36},{5,37},{6,38},{7,39},{8,40},{9,... | collective-permute-start | bytes 1216520 | tf_op jit(solution)/shard_map/ppermute | solution.py:248
  549.0 12.7 %collective-permute-start.55 = (bf16[66,1536]{1,0:T(8,128)(2,1)S(1)}, bf16[66,1536]{1,0:T(8,128)(2,1)S(1)}, u32[]{:S(2)}, u32[]{:S(2)}) collective-permute-start(bf16[66,1536]{1,0:T(8,128)(2,1)S(1)} %get-tuple-element.244), channel_id=1, source_target_pairs={{64,60},{65,61},{66,62},{67,63},{68,56},{69,57},{70,58},{71,59},{7... | collective-permute-start | bytes 608264 | tf_op jit(solution)/shard_map/ppermute | solution.py:248
  562.2 14.4 %collective-permute-start.57 = (bf16[2,66,1536]{2,1,0:T(8,128)(2,1)S(1)}, bf16[2,66,1536]{2,1,0:T(8,128)(2,1)S(1)}, u32[]{:S(2)}, u32[]{:S(2)}) collective-permute-start(bf16[2,66,1536]{2,1,0:T(8,128)(2,1)S(1)} %shard_map.117.refs_4_), channel_id=1, source_target_pairs={{33,32},{34,33},{35,34},{32,35},{37,36},{38,37},{39,38},{36,39},{4... | collective-permute-start | bytes 1216520 | tf_op jit(solution)/shard_map/ppermute | solution.py:374
  566.6 10.7 %collective-permute-start.58 = (bf16[2,66,1536]{2,1,0:T(8,128)(2,1)S(1)}, bf16[2,66,1536]{2,1,0:T(8,128)(2,1)S(1)}, u32[]{:S(2)}, u32[]{:S(2)}) collective-permute-start(bf16[2,66,1536]{2,1,0:T(8,128)(2,1)S(1)} %shard_map.117.refs_4_), channel_id=1, source_target_pairs={{34,32},{35,33},{32,34},{33,35},{38,36},{39,37},{36,38},{37,39},{4... | collective-permute-start | bytes 1216520 | tf_op jit(solution)/shard_map/ppermute | solution.py:374
  569.1 12.9 %collective-permute-start.59 = (bf16[2,66,1536]{2,1,0:T(8,128)(2,1)S(1)}, bf16[2,66,1536]{2,1,0:T(8,128)(2,1)S(1)}, u32[]{:S(2)}, u32[]{:S(2)}) collective-permute-start(bf16[2,66,1536]{2,1,0:T(8,128)(2,1)S(1)} %shard_map.117.refs_4_), channel_id=1, source_target_pairs={{35,32},{32,33},{33,34},{34,35},{39,36},{36,37},{37,38},{38,39},{4... | collective-permute-start | bytes 1216520 | tf_op jit(solution)/shard_map/ppermute | solution.py:374
  588.6 10.1 %collective-permute-start.61 = (bf16[4,24,1536]{2,1,0:T(8,128)(2,1)S(1)}, bf16[4,24,1536]{2,1,0:T(8,128)(2,1)S(1)}, u32[]{:S(2)}, u32[]{:S(2)}) collective-permute-start(bf16[4,24,1536]{2,1,0:T(8,128)(2,1)S(1)} %dynamic-slice_convert_fusion), channel_id=1, source_target_pairs={{0,4},{1,5},{2,6},{3,7},{4,0},{5,1},{6,2},{7,3},{8,12},{9,13},{10,... | collective-permute-start | bytes 884744 | tf_op jit(solution)/shard_map/ppermute | solution.py:441
  598.8 11.7 %collective-permute-start.62 = (bf16[2,24,1536]{2,1,0:T(8,128)(2,1)S(1)}, bf16[2,24,1536]{2,1,0:T(8,128)(2,1)S(1)}, u32[]{:S(2)}, u32[]{:S(2)}) collective-permute-start(bf16[2,24,1536]{2,1,0:T(8,128)(2,1)S(1)} %dynamic-slice_convert_fusion.1), channel_id=1, source_target_pairs={{0,8},{1,9},{2,10},{3,11},{4,12},{5,13},{6,14},{7,15},{8,0},{9,1},... | collective-permute-start | bytes 442376 | tf_op jit(solution)/shard_map/ppermute | solution.py:441
  610.5 12.1 %collective-permute-start.63 = (bf16[1,24,1536]{2,1,0:T(8,128)(2,1)S(1)}, bf16[1,24,1536]{2,1,0:T(8,128)(2,1)S(1)}, u32[]{:S(2)}, u32[]{:S(2)}) collective-permute-start(bf16[1,24,1536]{2,1,0:T(8,128)(2,1)S(1)} %dynamic-slice_convert_fusion.2), channel_id=1, source_target_pairs={{0,16},{1,17},{2,18},{3,19},{4,20},{5,21},{6,22},{7,23},{8,24},{9,... | collective-permute-start | bytes 221192 | tf_op jit(solution)/shard_map/ppermute | solution.py:441
  (40 other events, 128.7 us)

commit v4 on v3

--- a/solution.py
+++ b/solution.py
@@ -255,14 +255,10 @@
     to_base = [(2 * block + 1, 2 * block) for block in range(block_count)]
     to_control = [(2 * block, 2 * block + 1) for block in range(block_count)]
 
+    shared_span = max(block_count // 2, chunk_count + 2)
+
     def forward_hops(step):
-        last = block_count + chunk_count - 2
-        if step < 3:
-            steps = range(3)
-        elif step > last - 3:
-            steps = range(last - 2, last + 1)
-        else:
-            steps = (step,)
+        steps = range(step % shared_span, block_count + chunk_count - 1, shared_span)
         return sorted(
             {
                 (2 * block + 1 - lag, 2 * block + 3 - lag)
@@ -274,13 +270,7 @@
         )
 
     def backward_hops(step):
-        last = block_count + chunk_count - 3
-        if step < 3:
-            steps = range(3)
-        elif step > last - 2:
-            steps = range(last - 1, last + 1)
-        else:
-            steps = (step,)
+        steps = range(step % shared_span, block_count + chunk_count - 2, shared_span)
         return sorted(
             {
                 (

time: 625 us -> 566 us (0.906)
  waiting for transfers between devices: 376 us -> 281 us
  starting transfers between devices: 142 us -> 178 us
    ppermute x55, waiting for transfers between devices: 334 us -> 239 us  [move(): return lax.ppermute(value, both_axes, pairs)]
    ppermute x55, starting transfers between devices: 117 us -> 153 us  [move(): return lax.ppermute(value, both_axes, pairs)]
  transfers between devices with their start and end apart: 64 -> 64, of which waited for: 29 -> 30; matrix products, arithmetic and copies ran while one was open for 2% -> 2% of each run, Pallas kernels for 2% -> 3%
where the time goes in v4:
time: 566 us; the launch traced here: 565 us
  waiting for transfers between devices  281 us (50%)
  starting transfers between devices  178 us (31%)
  Pallas kernels  84.9 us (15%)
  local copies, waits for them, and re-layouts  13.9 us (2%)
    ppermute x55, waiting for transfers between devices, move(): return lax.ppermute(value, both_axes, pairs)  239 us
    ppermute x55, starting transfers between devices, move(): return lax.ppermute(value, both_axes, pairs)  153 us
    pallas_call x55, Pallas kernels, local_call(): pl.pallas_call(kernel, out_shape=results, in_specs=[in_smem] + [in_vmem]...  84.9 us
    ppermute x3, waiting for transfers between devices, body(): lax.ppermute(sent.astype(jnp.bfloat16), 'dp', pairs).astype(jnp.float32)  27.4 us
    ppermute x6, starting transfers between devices, along_x(): return lax.ppermute(value, both_axes, pairs)  18.7 us
    ppermute x6, waiting for transfers between devices, along_x(): return lax.ppermute(value, both_axes, pairs)  14.9 us
  transfers between devices with their start and end apart: 64, of which 30 were waited for; matrix products, arithmetic and copies ran while one was open for 2% of the time, Pallas kernels for 3%

profile of v4, /device:TPU:1, one launch (start us, length us, event | category | flops | bytes accessed | tf_op | source)
XLA Modules:
  0.0 564.9 jit_solution(17463838628001763048)
XLA Ops:
  0.0 16.3 %collective-permute-start.4 = (bf16[768,1536]{1,0:T(8,128)(2,1)}, bf16[768,1536]{1,0:T(8,128)(2,1)S(1)}, u32[]{:S(2)}, u32[]{:S(2)}) collective-permute-start(bf16[768,1536]{1,0:T(8,128)(2,1)} %bitcast.39), channel_id=1, source_target_pairs={{32,0},{33,1},{34,2},{35,3},{36,4},{37,5},{38,6},{39,7},{40,8},{41... | collective-permute-start | bytes 7077896 | tf_op jit(solution)/shard_map/ppermute | solution.py:248
  34.0 5.3 collective-permute-start.2
  42.3 6.9 %collective-permute-done.2.refs_1_ = bf16[66,1536]{1,0:T(8,128)(2,1)S(1)} collective-permute-done((bf16[66,1536]{1,0:T(8,128)(2,1)S(1)}, bf16[66,1536]{1,0:T(8,128)(2,1)S(1)}, u32[]{:S(2)}, u32[]{:S(2)}) %collective-permute-start.2) | collective-permute-done | bytes 202784 | tf_op jit(solution)/shard_map/ppermute | solution.py:248
  55.0 5.0 collective-permute-start.5
  60.6 10.6 %collective-permute-done.5.refs_1_ = bf16[66,1536]{1,0:T(8,128)(2,1)S(1)} collective-permute-done((bf16[66,1536]{1,0:T(8,128)(2,1)S(1)}, bf16[66,1536]{1,0:T(8,128)(2,1)S(1)}, u32[]{:S(2)}, u32[]{:S(2)}) %collective-permute-start.5) | collective-permute-done | bytes 202784 | tf_op jit(solution)/shard_map/ppermute | solution.py:248
  74.9 5.7 %collective-permute-start = (bf16[66,1536]{1,0:T(8,128)(2,1)S(1)}, bf16[66,1536]{1,0:T(8,128)(2,1)S(1)}, u32[]{:S(2)}, u32[]{:S(2)}) collective-permute-start(bf16[66,1536]{1,0:T(8,128)(2,1)S(1)} %copy-done.7), channel_id=1, source_target_pairs={{32,124},{33,125},{34,126},{35,127},{36,120},{37,121},{38,122},{39... | collective-permute-start | bytes 608264 | tf_op jit(solution)/shard_map/ppermute | solution.py:248
  85.0 17.5 %collective-permute-start.10 = (bf16[66,1536]{1,0:T(8,128)(2,1)S(1)}, bf16[66,1536]{1,0:T(8,128)(2,1)S(1)}, u32[]{:S(2)}, u32[]{:S(2)}) collective-permute-start(bf16[66,1536]{1,0:T(8,128)(2,1)S(1)} %get-tuple-element.142.outgoing), channel_id=1, source_target_pairs={{32,0},{33,1},{34,2},{35,3},{36,4},{37,5},{38,6},{39,7},{40,8},{41... | collective-permute-start | bytes 608264 | tf_op jit(solution)/shard_map/ppermute | solution.py:248
  105.9 3.9 collective-permute-start.12
  113.2 3.9 collective-permute-start.14
  120.5 3.9 collective-permute-start.16
  127.8 3.9 collective-permute-start.18
  135.1 3.9 collective-permute-start.20
  139.0 6.1 %collective-permute-start.19 = (bf16[66,1536]{1,0:T(8,128)(2,1)S(1)}, bf16[66,1536]{1,0:T(8,128)(2,1)S(1)}, u32[]{:S(2)}, u32[]{:S(2)}) collective-permute-start(bf16[66,1536]{1,0:T(8,128)(2,1)S(1)} %get-tuple-element.163.outgoing), channel_id=1, source_target_pairs={{32,124},{33,125},{34,126},{35,127},{36,120},{37,121},{38,122},{39... | collective-permute-start | bytes 608264 | tf_op jit(solution)/shard_map/ppermute | solution.py:248
  145.6 18.0 %collective-permute-done.19.refs_1_ = bf16[66,1536]{1,0:T(8,128)(2,1)S(1)} collective-permute-done((bf16[66,1536]{1,0:T(8,128)(2,1)S(1)}, bf16[66,1536]{1,0:T(8,128)(2,1)S(1)}, u32[]{:S(2)}, u32[]{:S(2)}) %collective-permute-start.19) | collective-permute-done | bytes 202784 | tf_op jit(solution)/shard_map/ppermute | solution.py:248
  166.6 5.3 collective-permute-start.21
  181.2 4.7 collective-permute-start.26
  189.3 3.9 collective-permute-start.28
  196.8 3.9 collective-permute-start.30
  204.1 3.9 collective-permute-start.32
  218.6 3.9 collective-permute-start.35
  222.5 15.9 %collective-permute-start.36 = (bf16[66,1536]{1,0:T(8,128)(2,1)S(1)}, bf16[66,1536]{1,0:T(8,128)(2,1)S(1)}, u32[]{:S(2)}, u32[]{:S(2)}) collective-permute-start(bf16[66,1536]{1,0:T(8,128)(2,1)S(1)} %get-tuple-element.195.outgoing), channel_id=1, source_target_pairs={{32,124},{33,125},{34,126},{35,127},{36,120},{37,121},{38,122},{39... | collective-permute-start | bytes 608264 | tf_op jit(solution)/shard_map/ppermute | solution.py:248
  266.2 94.8 %collective-permute-done.43.refs_1_ = bf16[66,1536]{1,0:T(8,128)(2,1)S(1)} collective-permute-done((bf16[66,1536]{1,0:T(8,128)(2,1)S(1)}, bf16[66,1536]{1,0:T(8,128)(2,1)S(1)}, u32[]{:S(2)}, u32[]{:S(2)}) %collective-permute-start.43) | collective-permute-done | bytes 202784 | tf_op jit(solution)/shard_map/ppermute | solution.py:248
  364.7 7.2 %collective-permute-done.44.refs_1_ = bf16[66,1536]{1,0:T(8,128)(2,1)S(1)} collective-permute-done((bf16[66,1536]{1,0:T(8,128)(2,1)S(1)}, bf16[66,1536]{1,0:T(8,128)(2,1)S(1)}, u32[]{:S(2)}, u32[]{:S(2)}) %collective-permute-start.44) | collective-permute-done | bytes 202784 | tf_op jit(solution)/shard_map/ppermute | solution.py:248
  376.6 4.4 collective-permute-start.45
  408.9 82.2 %collective-permute-done.54.refs_1_ = bf16[66,1536]{1,0:T(8,128)(2,1)S(1)} collective-permute-done((bf16[66,1536]{1,0:T(8,128)(2,1)S(1)}, bf16[66,1536]{1,0:T(8,128)(2,1)S(1)}, u32[]{:S(2)}, u32[]{:S(2)}) %collective-permute-start.54) | collective-permute-done | bytes 202784 | tf_op jit(solution)/shard_map/ppermute | solution.py:248
  496.0 7.2 %collective-permute-done.55.arrived = bf16[66,1536]{1,0:T(8,128)(2,1)S(1)} collective-permute-done((bf16[66,1536]{1,0:T(8,128)(2,1)S(1)}, bf16[66,1536]{1,0:T(8,128)(2,1)S(1)}, u32[]{:S(2)}, u32[]{:S(2)}) %collective-permute-start.55) | collective-permute-done | bytes 202784 | tf_op jit(solution)/shard_map/ppermute | solution.py:248
  503.8 4.4 collective-permute-start.57
  513.1 5.0 collective-permute-done.57.refs_5_
  518.8 4.6 collective-permute-done.59.refs_7_
  532.1 8.1 %collective-permute-done.61 = bf16[4,24,1536]{2,1,0:T(8,128)(2,1)S(1)} collective-permute-done((bf16[4,24,1536]{2,1,0:T(8,128)(2,1)S(1)}, bf16[4,24,1536]{2,1,0:T(8,128)(2,1)S(1)}, u32[]{:S(2)}, u32[]{:S(2)}) %collective-permute-start.61) | collective-permute-done | bytes 294944 | tf_op jit(solution)/shard_map/ppermute | solution.py:431
  542.3 9.7 %collective-permute-done.62 = bf16[2,24,1536]{2,1,0:T(8,128)(2,1)S(1)} collective-permute-done((bf16[2,24,1536]{2,1,0:T(8,128)(2,1)S(1)}, bf16[2,24,1536]{2,1,0:T(8,128)(2,1)S(1)}, u32[]{:S(2)}, u32[]{:S(2)}) %collective-permute-start.62) | collective-permute-done | bytes 147488 | tf_op jit(solution)/shard_map/ppermute | solution.py:431
  554.6 9.6 %collective-permute-done.63 = bf16[1,24,1536]{2,1,0:T(8,128)(2,1)S(1)} collective-permute-done((bf16[1,24,1536]{2,1,0:T(8,128)(2,1)S(1)}, bf16[1,24,1536]{2,1,0:T(8,128)(2,1)S(1)}, u32[]{:S(2)}, u32[]{:S(2)}) %collective-permute-start.63) | collective-permute-done | bytes 73760 | tf_op jit(solution)/shard_map/ppermute | solution.py:431
  (198 shorter events, 173.9 us)
Async XLA Ops:
  0.0 41.7 %collective-permute-start.4 = (bf16[768,1536]{1,0:T(8,128)(2,1)}, bf16[768,1536]{1,0:T(8,128)(2,1)S(1)}, u32[]{:S(2)}, u32[]{:S(2)}) collective-permute-start(bf16[768,1536]{1,0:T(8,128)(2,1)} %bitcast.39), channel_id=1, source_target_pairs={{32,0},{33,1},{34,2},{35,3},{36,4},{37,5},{38,6},{39,7},{40,8},{41... | collective-permute-start | bytes 7077896 | tf_op jit(solution)/shard_map/ppermute | solution.py:248
  34.0 15.3 %collective-permute-start.2 = (bf16[66,1536]{1,0:T(8,128)(2,1)S(1)}, bf16[66,1536]{1,0:T(8,128)(2,1)S(1)}, u32[]{:S(2)}, u32[]{:S(2)}) collective-permute-start(bf16[66,1536]{1,0:T(8,128)(2,1)S(1)} %get-tuple-element.130.outgoing), channel_id=1, source_target_pairs={{32,124},{33,125},{34,126},{35,127},{36,120},{37,121},{38,122},{39... | collective-permute-start | bytes 608264 | tf_op jit(solution)/shard_map/ppermute | solution.py:248
  53.4 6.6 %collective-permute-start.6 = (bf16[66,1536]{1,0:T(8,128)(2,1)S(1)}, bf16[66,1536]{1,0:T(8,128)(2,1)S(1)}, u32[]{:S(2)}, u32[]{:S(2)}) collective-permute-start(bf16[66,1536]{1,0:T(8,128)(2,1)S(1)} %get-tuple-element.134.outgoing), channel_id=1, source_target_pairs={{32,0},{33,1},{34,2},{35,3},{36,4},{37,5},{38,6},{39,7},{40,8},{41... | collective-permute-start | bytes 608264 | tf_op jit(solution)/shard_map/ppermute | solution.py:248
  55.0 16.2 %collective-permute-start.5 = (bf16[66,1536]{1,0:T(8,128)(2,1)S(1)}, bf16[66,1536]{1,0:T(8,128)(2,1)S(1)}, u32[]{:S(2)}, u32[]{:S(2)}) collective-permute-start(bf16[66,1536]{1,0:T(8,128)(2,1)S(1)} %get-tuple-element.134.outgoing), channel_id=1, source_target_pairs={{0,92},{1,93},{2,94},{3,95},{4,88},{5,89},{6,90},{7,91},{8,84},{9,... | collective-permute-start | bytes 608264 | tf_op jit(solution)/shard_map/ppermute | solution.py:248
  72.9 9.1 %collective-permute-start.8 = (bf16[66,1536]{1,0:T(8,128)(2,1)S(1)}, bf16[66,1536]{1,0:T(8,128)(2,1)S(1)}, u32[]{:S(2)}, u32[]{:S(2)}) collective-permute-start(bf16[66,1536]{1,0:T(8,128)(2,1)S(1)} %get-tuple-element.138.outgoing), channel_id=1, source_target_pairs={{32,0},{33,1},{34,2},{35,3},{36,4},{37,5},{38,6},{39,7},{40,8},{41... | collective-permute-start | bytes 608264 | tf_op jit(solution)/shard_map/ppermute | solution.py:248
  74.3 8.3 %collective-permute-start.7 = (bf16[66,1536]{1,0:T(8,128)(2,1)S(1)}, bf16[66,1536]{1,0:T(8,128)(2,1)S(1)}, u32[]{:S(2)}, u32[]{:S(2)}) collective-permute-start(bf16[66,1536]{1,0:T(8,128)(2,1)S(1)} %get-tuple-element.138.outgoing), channel_id=1, source_target_pairs={{0,92},{1,93},{2,94},{3,95},{4,88},{5,89},{6,90},{7,91},{8,84},{9,... | collective-permute-start | bytes 608264 | tf_op jit(solution)/shard_map/ppermute | solution.py:248
  74.9 27.6 %collective-permute-start = (bf16[66,1536]{1,0:T(8,128)(2,1)S(1)}, bf16[66,1536]{1,0:T(8,128)(2,1)S(1)}, u32[]{:S(2)}, u32[]{:S(2)}) collective-permute-start(bf16[66,1536]{1,0:T(8,128)(2,1)S(1)} %copy-done.7), channel_id=1, source_target_pairs={{32,124},{33,125},{34,126},{35,127},{36,120},{37,121},{38,122},{39... | collective-permute-start | bytes 608264 | tf_op jit(solution)/shard_map/ppermute | solution.py:248
  80.7 21.9 %collective-permute-start.1 = (bf16[66,1536]{1,0:T(8,128)(2,1)S(1)}, bf16[66,1536]{1,0:T(8,128)(2,1)S(1)}, u32[]{:S(2)}, u32[]{:S(2)}) collective-permute-start(bf16[66,1536]{1,0:T(8,128)(2,1)S(1)} %copy-done.6), channel_id=1, source_target_pairs={{32,124},{33,125},{34,126},{35,127},{36,120},{37,121},{38,122},{39... | collective-permute-start | bytes 608264 | tf_op jit(solution)/shard_map/ppermute | solution.py:248
  84.3 18.2 %collective-permute-start.9 = (bf16[66,1536]{1,0:T(8,128)(2,1)S(1)}, bf16[66,1536]{1,0:T(8,128)(2,1)S(1)}, u32[]{:S(2)}, u32[]{:S(2)}) collective-permute-start(bf16[66,1536]{1,0:T(8,128)(2,1)S(1)} %get-tuple-element.142.outgoing), channel_id=1, source_target_pairs={{64,156},{65,157},{66,158},{67,159},{68,152},{69,153},{70,154},{71... | collective-permute-start | bytes 608264 | tf_op jit(solution)/shard_map/ppermute | solution.py:248
  85.0 18.6 %collective-permute-start.10 = (bf16[66,1536]{1,0:T(8,128)(2,1)S(1)}, bf16[66,1536]{1,0:T(8,128)(2,1)S(1)}, u32[]{:S(2)}, u32[]{:S(2)}) collective-permute-start(bf16[66,1536]{1,0:T(8,128)(2,1)S(1)} %get-tuple-element.142.outgoing), channel_id=1, source_target_pairs={{32,0},{33,1},{34,2},{35,3},{36,4},{37,5},{38,6},{39,7},{40,8},{41... | collective-permute-start | bytes 608264 | tf_op jit(solution)/shard_map/ppermute | solution.py:248
  135.1 10.0 %collective-permute-start.20 = (bf16[66,1536]{1,0:T(8,128)(2,1)S(1)}, bf16[66,1536]{1,0:T(8,128)(2,1)S(1)}, u32[]{:S(2)}, u32[]{:S(2)}) collective-permute-start(bf16[66,1536]{1,0:T(8,128)(2,1)S(1)} %get-tuple-element.163.outgoing), channel_id=1, source_target_pairs={{32,0},{33,1},{34,2},{35,3},{36,4},{37,5},{38,6},{39,7},{40,8},{41... | collective-permute-start | bytes 608264 | tf_op jit(solution)/shard_map/ppermute | solution.py:248
  139.0 24.6 %collective-permute-start.19 = (bf16[66,1536]{1,0:T(8,128)(2,1)S(1)}, bf16[66,1536]{1,0:T(8,128)(2,1)S(1)}, u32[]{:S(2)}, u32[]{:S(2)}) collective-permute-start(bf16[66,1536]{1,0:T(8,128)(2,1)S(1)} %get-tuple-element.163.outgoing), channel_id=1, source_target_pairs={{32,124},{33,125},{34,126},{35,127},{36,120},{37,121},{38,122},{39... | collective-permute-start | bytes 608264 | tf_op jit(solution)/shard_map/ppermute | solution.py:248
  165.3 6.6 %collective-permute-start.22 = (bf16[66,1536]{1,0:T(8,128)(2,1)S(1)}, bf16[66,1536]{1,0:T(8,128)(2,1)S(1)}, u32[]{:S(2)}, u32[]{:S(2)}) collective-permute-start(bf16[66,1536]{1,0:T(8,128)(2,1)S(1)} %get-tuple-element.167.outgoing), channel_id=1, source_target_pairs={{32,0},{33,1},{34,2},{35,3},{36,4},{37,5},{38,6},{39,7},{40,8},{41... | collective-permute-start | bytes 608264 | tf_op jit(solution)/shard_map/ppermute | solution.py:248
  166.6 8.2 %collective-permute-start.21 = (bf16[66,1536]{1,0:T(8,128)(2,1)S(1)}, bf16[66,1536]{1,0:T(8,128)(2,1)S(1)}, u32[]{:S(2)}, u32[]{:S(2)}) collective-permute-start(bf16[66,1536]{1,0:T(8,128)(2,1)S(1)} %get-tuple-element.167.outgoing), channel_id=1, source_target_pairs={{0,92},{1,93},{2,94},{3,95},{4,88},{5,89},{6,90},{7,91},{8,84},{9,... | collective-permute-start | bytes 608264 | tf_op jit(solution)/shard_map/ppermute | solution.py:248
  181.2 5.8 %collective-permute-start.26 = (bf16[66,1536]{1,0:T(8,128)(2,1)S(1)}, bf16[66,1536]{1,0:T(8,128)(2,1)S(1)}, u32[]{:S(2)}, u32[]{:S(2)}) collective-permute-start(bf16[66,1536]{1,0:T(8,128)(2,1)S(1)} %get-tuple-element.175.outgoing), channel_id=1, source_target_pairs={{32,0},{33,1},{34,2},{35,3},{36,4},{37,5},{38,6},{39,7},{40,8},{41... | collective-permute-start | bytes 608264 | tf_op jit(solution)/shard_map/ppermute | solution.py:248
  218.6 19.8 %collective-permute-start.35 = (bf16[66,1536]{1,0:T(8,128)(2,1)S(1)}, bf16[66,1536]{1,0:T(8,128)(2,1)S(1)}, u32[]{:S(2)}, u32[]{:S(2)}) collective-permute-start(bf16[66,1536]{1,0:T(8,128)(2,1)S(1)} %get-tuple-element.195.outgoing), channel_id=1, source_target_pairs={{32,0},{33,1},{34,2},{35,3},{36,4},{37,5},{38,6},{39,7},{40,8},{41... | collective-permute-start | bytes 608264 | tf_op jit(solution)/shard_map/ppermute | solution.py:248
  222.5 18.7 %collective-permute-start.36 = (bf16[66,1536]{1,0:T(8,128)(2,1)S(1)}, bf16[66,1536]{1,0:T(8,128)(2,1)S(1)}, u32[]{:S(2)}, u32[]{:S(2)}) collective-permute-start(bf16[66,1536]{1,0:T(8,128)(2,1)S(1)} %get-tuple-element.195.outgoing), channel_id=1, source_target_pairs={{32,124},{33,125},{34,126},{35,127},{36,120},{37,121},{38,122},{39... | collective-permute-start | bytes 608264 | tf_op jit(solution)/shard_map/ppermute | solution.py:248
  264.9 96.1 %collective-permute-start.43 = (bf16[66,1536]{1,0:T(8,128)(2,1)S(1)}, bf16[66,1536]{1,0:T(8,128)(2,1)S(1)}, u32[]{:S(2)}, u32[]{:S(2)}) collective-permute-start(bf16[66,1536]{1,0:T(8,128)(2,1)S(1)} %get-tuple-element.215), channel_id=1, source_target_pairs={{64,60},{65,61},{66,62},{67,63},{68,56},{69,57},{70,58},{71,59},{7... | collective-permute-start | bytes 608264 | tf_op jit(solution)/shard_map/ppermute | solution.py:248
  363.3 8.6 %collective-permute-start.44 = (bf16[66,1536]{1,0:T(8,128)(2,1)S(1)}, bf16[66,1536]{1,0:T(8,128)(2,1)S(1)}, u32[]{:S(2)}, u32[]{:S(2)}) collective-permute-start(bf16[66,1536]{1,0:T(8,128)(2,1)S(1)} %get-tuple-element.217), channel_id=1, source_target_pairs={{64,60},{65,61},{66,62},{67,63},{68,56},{69,57},{70,58},{71,59},{7... | collective-permute-start | bytes 608264 | tf_op jit(solution)/shard_map/ppermute | solution.py:248
  374.2 16.4 %collective-permute-start.48 = (bf16[66,1536]{1,0:T(8,128)(2,1)S(1)}, bf16[66,1536]{1,0:T(8,128)(2,1)S(1)}, u32[]{:S(2)}, u32[]{:S(2)}) collective-permute-start(bf16[66,1536]{1,0:T(8,128)(2,1)S(1)} %get-tuple-element.219), channel_id=1, source_target_pairs={{448,412},{449,413},{450,414},{451,415},{452,408},{453,409},{454,4... | collective-permute-start | bytes 608264 | tf_op jit(solution)/shard_map/ppermute | solution.py:248
  376.6 9.4 %collective-permute-start.45 = (bf16[2,2,66,192]{3,2,1,0:T(8,128)(2,1)S(1)}, bf16[2,2,66,192]{3,2,1,0:T(8,128)(2,1)S(1)}, u32[]{:S(2)}, u32[]{:S(2)}) collective-permute-start(bf16[2,2,66,192]{3,2,1,0:T(8,128)(2,1)S(1)} %get-tuple-element.223), channel_id=1, source_target_pairs={{33,32},{34,33},{35,34},{32,35},{37,36},{38,37},{39,38},{36,39},{4... | collective-permute-start | bytes 304136 | tf_op jit(solution)/shard_map/ppermute | solution.py:364
  381.0 7.4 %collective-permute-start.46 = (bf16[2,2,66,192]{3,2,1,0:T(8,128)(2,1)S(1)}, bf16[2,2,66,192]{3,2,1,0:T(8,128)(2,1)S(1)}, u32[]{:S(2)}, u32[]{:S(2)}) collective-permute-start(bf16[2,2,66,192]{3,2,1,0:T(8,128)(2,1)S(1)} %get-tuple-element.224), channel_id=1, source_target_pairs={{34,32},{35,33},{32,34},{33,35},{38,36},{39,37},{36,38},{37,39},{4... | collective-permute-start | bytes 304136 | tf_op jit(solution)/shard_map/ppermute | solution.py:364
  383.4 7.1 %collective-permute-start.47 = (bf16[2,2,66,192]{3,2,1,0:T(8,128)(2,1)S(1)}, bf16[2,2,66,192]{3,2,1,0:T(8,128)(2,1)S(1)}, u32[]{:S(2)}, u32[]{:S(2)}) collective-permute-start(bf16[2,2,66,192]{3,2,1,0:T(8,128)(2,1)S(1)} %get-tuple-element.225), channel_id=1, source_target_pairs={{35,32},{32,33},{33,34},{34,35},{39,36},{36,37},{37,38},{38,39},{4... | collective-permute-start | bytes 304136 | tf_op jit(solution)/shard_map/ppermute | solution.py:364
  407.6 83.5 %collective-permute-start.54 = (bf16[66,1536]{1,0:T(8,128)(2,1)S(1)}, bf16[66,1536]{1,0:T(8,128)(2,1)S(1)}, u32[]{:S(2)}, u32[]{:S(2)}) collective-permute-start(bf16[66,1536]{1,0:T(8,128)(2,1)S(1)} %get-tuple-element.242), channel_id=1, source_target_pairs={{64,60},{65,61},{66,62},{67,63},{68,56},{69,57},{70,58},{71,59},{7... | collective-permute-start | bytes 608264 | tf_op jit(solution)/shard_map/ppermute | solution.py:248
  493.4 9.8 %collective-permute-start.56 = (bf16[2,66,1536]{2,1,0:T(8,128)(2,1)S(1)}, bf16[2,66,1536]{2,1,0:T(8,128)(2,1)S(1)}, u32[]{:S(2)}, u32[]{:S(2)}) collective-permute-start(bf16[2,66,1536]{2,1,0:T(8,128)(2,1)S(1)} %get-tuple-element.245.kept), channel_id=1, source_target_pairs={{0,32},{1,33},{2,34},{3,35},{4,36},{5,37},{6,38},{7,39},{8,40},{9,... | collective-permute-start | bytes 1216520 | tf_op jit(solution)/shard_map/ppermute | solution.py:248
  494.7 8.5 %collective-permute-start.55 = (bf16[66,1536]{1,0:T(8,128)(2,1)S(1)}, bf16[66,1536]{1,0:T(8,128)(2,1)S(1)}, u32[]{:S(2)}, u32[]{:S(2)}) collective-permute-start(bf16[66,1536]{1,0:T(8,128)(2,1)S(1)} %get-tuple-element.244), channel_id=1, source_target_pairs={{64,60},{65,61},{66,62},{67,63},{68,56},{69,57},{70,58},{71,59},{7... | collective-permute-start | bytes 608264 | tf_op jit(solution)/shard_map/ppermute | solution.py:248
  503.8 14.4 %collective-permute-start.57 = (bf16[2,66,1536]{2,1,0:T(8,128)(2,1)S(1)}, bf16[2,66,1536]{2,1,0:T(8,128)(2,1)S(1)}, u32[]{:S(2)}, u32[]{:S(2)}) collective-permute-start(bf16[2,66,1536]{2,1,0:T(8,128)(2,1)S(1)} %shard_map.117.refs_4_), channel_id=1, source_target_pairs={{33,32},{34,33},{35,34},{32,35},{37,36},{38,37},{39,38},{36,39},{4... | collective-permute-start | bytes 1216520 | tf_op jit(solution)/shard_map/ppermute | solution.py:364
  508.2 10.7 %collective-permute-start.58 = (bf16[2,66,1536]{2,1,0:T(8,128)(2,1)S(1)}, bf16[2,66,1536]{2,1,0:T(8,128)(2,1)S(1)}, u32[]{:S(2)}, u32[]{:S(2)}) collective-permute-start(bf16[2,66,1536]{2,1,0:T(8,128)(2,1)S(1)} %shard_map.117.refs_4_), channel_id=1, source_target_pairs={{34,32},{35,33},{32,34},{33,35},{38,36},{39,37},{36,38},{37,39},{4... | collective-permute-start | bytes 1216520 | tf_op jit(solution)/shard_map/ppermute | solution.py:364
  510.6 12.8 %collective-permute-start.59 = (bf16[2,66,1536]{2,1,0:T(8,128)(2,1)S(1)}, bf16[2,66,1536]{2,1,0:T(8,128)(2,1)S(1)}, u32[]{:S(2)}, u32[]{:S(2)}) collective-permute-start(bf16[2,66,1536]{2,1,0:T(8,128)(2,1)S(1)} %shard_map.117.refs_4_), channel_id=1, source_target_pairs={{35,32},{32,33},{33,34},{34,35},{39,36},{36,37},{37,38},{38,39},{4... | collective-permute-start | bytes 1216520 | tf_op jit(solution)/shard_map/ppermute | solution.py:364
  530.1 10.1 %collective-permute-start.61 = (bf16[4,24,1536]{2,1,0:T(8,128)(2,1)S(1)}, bf16[4,24,1536]{2,1,0:T(8,128)(2,1)S(1)}, u32[]{:S(2)}, u32[]{:S(2)}) collective-permute-start(bf16[4,24,1536]{2,1,0:T(8,128)(2,1)S(1)} %dynamic-slice_convert_fusion), channel_id=1, source_target_pairs={{0,4},{1,5},{2,6},{3,7},{4,0},{5,1},{6,2},{7,3},{8,12},{9,13},{10,... | collective-permute-start | bytes 884744 | tf_op jit(solution)/shard_map/ppermute | solution.py:431
  540.3 11.7 %collective-permute-start.62 = (bf16[2,24,1536]{2,1,0:T(8,128)(2,1)S(1)}, bf16[2,24,1536]{2,1,0:T(8,128)(2,1)S(1)}, u32[]{:S(2)}, u32[]{:S(2)}) collective-permute-start(bf16[2,24,1536]{2,1,0:T(8,128)(2,1)S(1)} %dynamic-slice_convert_fusion.1), channel_id=1, source_target_pairs={{0,8},{1,9},{2,10},{3,11},{4,12},{5,13},{6,14},{7,15},{8,0},{9,1},... | collective-permute-start | bytes 442376 | tf_op jit(solution)/shard_map/ppermute | solution.py:431
  552.1 12.1 %collective-permute-start.63 = (bf16[1,24,1536]{2,1,0:T(8,128)(2,1)S(1)}, bf16[1,24,1536]{2,1,0:T(8,128)(2,1)S(1)}, u32[]{:S(2)}, u32[]{:S(2)}) collective-permute-start(bf16[1,24,1536]{2,1,0:T(8,128)(2,1)S(1)} %dynamic-slice_convert_fusion.2), channel_id=1, source_target_pairs={{0,16},{1,17},{2,18},{3,19},{4,20},{5,21},{6,22},{7,23},{8,24},{9,... | collective-permute-start | bytes 221192 | tf_op jit(solution)/shard_map/ppermute | solution.py:431
  (40 other events, 146.1 us)
